TPU v7x, 32 devices: a whole 2x2x4 slice. The times are simulated.
32 devices in a mesh: dp: 16 (over z, x, core), seq: 2 (over y).
Axes of the slice: x: 2, y: 2, z: 4, core: 2. Of those that a mesh axis runs over, the one named last changes fastest.
Arguments:
- dec_input: bfloat16 [64, 128, 768], P('dp', 'seq'), may hold values from -6 to 6
- memory: bfloat16 [64, 256, 768], P('dp', 'seq'), may hold values from -6 to 6
- src_len: int32 [64], P('dp'), may hold values from 128 to 256, as said below
- out_grad: bfloat16 [64, 128, 768], P('dp', 'seq'), may hold values from -6 to 6
- self_qkv: bfloat16 [768, 2304], replicated, may hold values from -0.21875 to 0.21875
- self_out: bfloat16 [768, 768], replicated, may hold values from -1.75 to 1.75
- cross_query: bfloat16 [768, 768], replicated, may hold values from -0.21875 to 0.21875
- cross_kv: bfloat16 [768, 1536], replicated, may hold values from -0.21875 to 0.21875
- cross_out: bfloat16 [768, 768], replicated, may hold values from -3.5 to 3.5
- ffn_in: bfloat16 [768, 3072], replicated, may hold values from -0.21875 to 0.21875
- ffn_out: bfloat16 [3072, 768], replicated, may hold values from -0.109375 to 0.109375
- norm_gain: float32 [3, 768], replicated, may hold values from 0.5 to 1.5
- norm_bias: float32 [3, 768], replicated, may hold values from -3 to 3
Outputs:
- layer_out: bfloat16 [64, 128, 768], P('dp', 'seq')
- input_grad: float32 [64, 128, 768], P('dp', 'seq')
- memory_grad: float32 [64, 256, 768], P('dp', 'seq')
- self_qkv_grad: float32 [768, 2304], P('dp', 'seq')
- self_out_grad: float32 [768, 768], P('dp', 'seq')
- cross_query_grad: float32 [768, 768], P('dp', 'seq')
- cross_kv_grad: float32 [768, 1536], P('dp', 'seq')
- cross_out_grad: float32 [768, 768], P('dp', 'seq')
- ffn_in_grad: float32 [768, 3072], P('dp', 'seq')
- ffn_out_grad: float32 [3072, 768], P('dp', 'seq')
- norm_gain_grad: float32 [3, 768], replicated
- norm_bias_grad: float32 [3, 768], replicated
Inputs may be any that keep to these rules, and one draw needn't show every extreme that they name: `src_len`: each source length is 256 or 128; every block of 4 consecutive examples holds at least one of each.
All inputs are finite; a program needn't handle non-finite values.
Results may differ from a plain program's by a relative error of at most 0.023.
Values may be sent and summed in bfloat16 or wider, within the bound.
A program may use at most 192 MiB of HBM per device.

v0:
```python
import functools
import math

import jax
import jax.numpy as jnp
from jax import lax
from jax.experimental import pallas as pl
from jax.experimental.pallas import tpu as pltpu
from jax.sharding import PartitionSpec as P

HEADS = 12
HEAD_DIM = 64
MESH = pl.DeviceIdType.MESH
F32 = jnp.float32
BF16 = jnp.bfloat16
TRIPLES = 16
ORDERS = (("x", "l", "y", "h"), ("y", "x", "l", "h"), ("l", "x", "y", "h"))


def place():
    i = lax.axis_index("dp")
    return {"c": i % 2, "x": (i // 2) % 2, "l": (i // 4) % 2, "h": i // 8, "y": lax.axis_index("seq")}


def partner(axis, at):
    i = lax.axis_index("dp")
    y = at["y"]
    if axis == "y":
        return (i, 1 - y)
    step = {"c": 1, "x": 2, "l": 4, "h": 8}[axis]
    return (i + step - 2 * step * at[axis], y)


def greet(at):
    barrier = pltpu.get_barrier_semaphore()
    for axis in ("c", "x", "l", "h", "y"):
        pl.semaphore_signal(barrier, inc=1, device_id=partner(axis, at), device_id_type=MESH)
    pl.semaphore_wait(barrier, 5)


def left_slot(t):
    return jnp.where(t < 4, t, jnp.where(t < 8, 4, jnp.where(t == 8, 5, jnp.where(t < 11, 6, jnp.where(t == 11, 8, jnp.where(t == 12, 9, 10))))))


def store_left(lt, slot, rows_by_feature):
    for i in range(16):
        lt[slot, i % 2, 48 * (i // 2) : 48 * (i // 2) + 48, :] = rows_by_feature[48 * i : 48 * i + 48, :]


class Reducer:
    SCRATCH = [
        pltpu.VMEM((2, 3, 384, 256), BF16),
        pltpu.VMEM((TRIPLES, 3, 384, 256), BF16),
        pltpu.VMEM((2, 3, 2, 2, 2, 2, 48, 128), BF16),
        pltpu.VMEM((TRIPLES, 3, 2, 2, 2, 48, 128), BF16),
        pltpu.VMEM((2, 3, 2, 2, 2, 48, 128), BF16),
        pltpu.VMEM((TRIPLES, 3, 2, 2, 48, 128), BF16),
        pltpu.VMEM((2, 3, 2, 2, 48, 128), BF16),
        pltpu.VMEM((TRIPLES, 3, 2, 48, 128), BF16),
        pltpu.VMEM((2, 3, 2, 48, 128), BF16),
        pltpu.VMEM((TRIPLES, 3, 48, 128), BF16),
        pltpu.SemaphoreType.DMA((5, 2, 3)),
        pltpu.SemaphoreType.DMA((5, TRIPLES, 3)),
    ]

    def __init__(self, at, lt, rg, out, s0, r0, s1, r1, s2, r2, s3, r3, s4, r4, send_sem, recv_sem):
        self.at, self.lt, self.rg, self.out = at, lt, rg, out
        self.sent, self.got = (s0, s1, s2, s3, s4), (r0, r1, r2, r3, r4)
        self.send_sem, self.recv_sem = send_sem, recv_sem

    def axis(self, stage, g):
        return "c" if stage == 0 else ORDERS[g][stage - 1]

    def copy(self, stage, t, g):
        axis = self.axis(stage, g)
        slot = t % 2
        src = self.sent[stage].at[slot, g]
        if stage:
            src = src.at[1 - self.at[axis]]
        return pltpu.make_async_remote_copy(
            src_ref=src,
            dst_ref=self.got[stage].at[t, g],
            send_sem=self.send_sem.at[stage, slot, g],
            recv_sem=self.recv_sem.at[stage, t, g],
            device_id=partner(axis, self.at),
            device_id_type=MESH,
        )

    def free(self, stage, t):
        @pl.when(t >= 2)
        def _():
            for g in range(3):
                self.copy(stage, t - 2, g).wait_send()

    def product(self, t, half, g):
        cols = slice(256 * g, 256 * g + 256)
        slot = left_slot(t)
        return jnp.dot(self.lt[slot, half], self.rg[t, :, cols], preferred_element_type=F32)

    def first(self, t):
        self.free(0, t)
        half = 1 - self.at["c"]
        memory = (t == 9) | (t == 10)
        for g in range(3):
            cols = slice(256 * g, 256 * g + 256)

            @pl.when(jnp.logical_not(memory))
            def _():
                self.sent[0][t % 2, g] = self.product(t, half, g).astype(BF16)

            @pl.when(memory)
            def _():
                more = jnp.dot(self.lt[7, half], self.rg[t + 7, :, cols], preferred_element_type=F32)
                self.sent[0][t % 2, g] = (self.product(t, half, g) + more).astype(BF16)

            self.copy(0, t, g).start()

    def second(self, t):
        self.free(1, t)
        half = self.at["c"]
        memory = (t == 9) | (t == 10)
        for g in range(3):
            cols = slice(256 * g, 256 * g + 256)
            self.copy(0, t, g).wait_recv()

            def spread(total):
                order = ORDERS[g]
                for b in range(8):
                    bits = {"h": b // 4, "l": (b // 2) % 2, "x": b % 2}
                    for y in range(2):
                        bits["y"] = y
                        where = tuple(bits[a] for a in order)
                        self.sent[1][(t % 2, g) + where] = total[48 * b : 48 * b + 48, 128 * y : 128 * y + 128].astype(BF16)

            @pl.when(jnp.logical_not(memory))
            def _():
                spread(self.product(t, half, g) + self.got[0][t, g].astype(F32))

            @pl.when(memory)
            def _():
                more = jnp.dot(self.lt[7, half], self.rg[t + 7, :, cols], preferred_element_type=F32)
                spread(self.product(t, half, g) + more + self.got[0][t, g].astype(F32))

            self.copy(1, t, g).start()

    def onward(self, stage, t):
        if stage < 5:
            self.free(stage, t)
        for g in range(3):
            self.copy(stage - 1, t, g).wait_recv()
            own = self.sent[stage - 1][t % 2, g, self.at[self.axis(stage - 1, g)]]
            total = own.astype(F32) + self.got[stage - 1][t, g].astype(F32)
            if stage < 5:
                self.sent[stage][t % 2, g] = total.astype(BF16)
                self.copy(stage, t, g).start()
            else:
                self.out[t, g] = total

    def tick(self, n):
        for stage in range(6):
            t = n - stage

            @pl.when((t >= 0) & (t < TRIPLES))
            def _():
                if stage == 0:
                    self.first(t)
                elif stage == 1:
                    self.second(t)
                else:
                    self.onward(stage, t)

    def drain(self):
        for stage in range(5):
            for t in (TRIPLES - 2, TRIPLES - 1):
                for g in range(3):
                    self.copy(stage, t, g).wait_send()


NORM_ORDER = ("c", "x", "y", "l", "h")


def norm_copy(j, at, own, got, send_sem, recv_sem):
    return pltpu.make_async_remote_copy(
        src_ref=own.at[j], dst_ref=got.at[j], send_sem=send_sem.at[j], recv_sem=recv_sem.at[j],
        device_id=partner(NORM_ORDER[j], at), device_id_type=MESH,
    )


def norm_step(j, at, own, got, send_sem, recv_sem):
    if j:
        norm_copy(j - 1, at, own, got, send_sem, recv_sem).wait()
        own[j] = own[j - 1] + got[j - 1]
    if j < 5:
        norm_copy(j, at, own, got, send_sem, recv_sem).start()


def assemble(units, first, count):
    block = units[first : first + count]
    return jnp.transpose(block, (2, 0, 1, 3)).reshape(48, count * 384)


def gather_outputs(units):
    ffn_out = jnp.transpose(units[0:4], (0, 2, 1, 3)).reshape(192, 384)
    return dict(ffn_out=ffn_out, ffn_in=assemble(units, 4, 4), cross_out=assemble(units, 8, 1), cross_kv=assemble(units, 9, 2),
                cross_query=assemble(units, 11, 1), self_out=assemble(units, 12, 1), self_qkv=assemble(units, 13, 3))


LANES = 128


def normed(v):
    center = jnp.mean(v, axis=-1, keepdims=True)
    centered = v - center
    spread = jnp.mean(centered * centered, axis=-1, keepdims=True)
    scale = lax.rsqrt(spread + 1e-05)
    return centered * scale, scale


def row_blocks(step, body):
    def run(b, carry):
        body(pl.ds(pl.multiple_of(b * step, step), step))
        return carry

    lax.fori_loop(0, 256 // step, run, 0)


def norm_forward(load, out, norm_gain, norm_bias, k):
    def body(rows):
        hat, _ = normed(load(rows))
        out[rows, :] = (hat * norm_gain[k : k + 1, :] + norm_bias[k : k + 1, :]).astype(BF16)

    row_blocks(64, body)


def norm_backward(load, load_grad, store, norm_gain, sums, k):
    def body(rows):
        hat, scale = normed(load(rows))
        dy = load_grad(rows)
        sums[k : k + 1, :] += jnp.sum(dy * hat, axis=0, keepdims=True)
        sums[k + 3 : k + 4, :] += jnp.sum(dy, axis=0, keepdims=True)
        dhat = dy * norm_gain[k : k + 1, :]
        mean = jnp.mean(dhat, axis=-1, keepdims=True)
        along = jnp.mean(dhat * hat, axis=-1, keepdims=True)
        store(rows, scale * (dhat - mean - hat * along))

    row_blocks(64, body)


def two_heads(tile):
    first = lax.broadcasted_iota(jnp.int32, tile.shape, 1) < HEAD_DIM
    zero = jnp.zeros_like(tile)
    return jnp.concatenate([jnp.where(first, tile, zero), jnp.where(first, zero, tile)], axis=0)


def side_by_side(stacked):
    rows = stacked.shape[0] // 2
    first = lax.broadcasted_iota(jnp.int32, (rows, stacked.shape[1]), 1) < HEAD_DIM
    return jnp.where(first, stacked[:rows], stacked[rows:])


def dot(a, b, over):
    return lax.dot_general(a, b, (over, ((), ())), preferred_element_type=F32)


LAST = ((1,), (1,))
PLAIN = ((1,), (0,))
ROWS = ((0,), (0,))


def attend(q, k, v, allowed):
    scores = jnp.where(allowed, dot(two_heads(q), k, LAST), -1e30)
    raised = jnp.exp(scores - jnp.max(scores, axis=-1, keepdims=True))
    weights = (raised * (1.0 / jnp.sum(raised, axis=-1, keepdims=True))).astype(BF16)
    return weights, side_by_side(dot(weights, v, PLAIN)).astype(BF16)


def attend_back(q, k, v, weights, dc):
    stacked = two_heads(dc)
    dv = dot(weights, stacked, ROWS)
    dweights = dot(stacked, v, LAST)
    probs = weights.astype(F32)
    terms = probs * dweights
    dscores = (terms - probs * jnp.sum(terms, axis=-1, keepdims=True)).astype(BF16)
    dq = side_by_side(dot(dscores, k, PLAIN)) * (1.0 / math.sqrt(HEAD_DIM))
    dk = dot(dscores, two_heads(q), ROWS)
    return dq.astype(BF16), dk.astype(BF16), dv.astype(BF16)


def column(slot, h, g):
    return (slot, slice(None), pl.ds(pl.multiple_of(256 * g + LANES * h, LANES), LANES))


def back(rg, slots, weight, rows=None):
    half = weight.shape[1] // 2
    total = None
    for j, slot in enumerate(slots):
        for g in range(3):
            at = j * 384 + g * LANES
            w = jnp.concatenate([weight[:, at : at + LANES], weight[:, half + at : half + at + LANES]], axis=1)
            term = dot(rg[slot, :, 256 * g : 256 * g + 256], w, LAST)
            total = term if total is None else total + term
    return total


def layer_kernel(
    dec_input, memory, src_len, out_grad, self_qkv, self_out, cross_query, cross_kv, cross_out, ffn_in, ffn_out,
    norm_gain, norm_bias,
    o_layer, o_input, o_memory, units, norm_out,
    x_in, mem, og, w_qkv, w_self, w_query, w_kv, w_cross, w_in, w_out,
    first, qkv, p_self, ctx_self, hidden1, second, qx, kv, p_cross, ctx_cross, hidden2, third,
    active, dup, acc, dthird,
    lt, rg, n_own, n_got, n_send, n_recv, load_sem, swap_send, swap_recv, out_sem, out_send, out_recv, *rest
):
    at = place()
    y = at["y"]
    red = Reducer(at, lt, rg, units, *rest)
    across = partner("y", at)

    loads = [
        pltpu.make_async_copy(src, dst, load_sem.at[n])
        for n, (src, dst) in enumerate(
            ((self_qkv, w_qkv), (self_out, w_self), (cross_kv, w_kv), (cross_query, w_query), (cross_out, w_cross))
        )
    ]
    for load in loads:
        load.start()

    def ffn_load(q):
        slot = q % 2
        cols = pl.ds(pl.multiple_of(q * 768, 768), 768)
        return (
            pltpu.make_async_copy(ffn_in.at[:, cols], w_in.at[slot], load_sem.at[7 + slot]),
            pltpu.make_async_copy(ffn_out.at[cols, :], w_out.at[slot], load_sem.at[9 + slot]),
        )

    for load in ffn_load(0):
        load.start()

    def own_rows(n, src, dst, rows):
        return [
            pltpu.make_async_copy(
                src.at[2 * y + e], dst.at[pl.ds(pl.multiple_of(2 * e * rows + y * rows, rows), rows), :], load_sem.at[11 + 2 * n + e]
            )
            for e in range(2)
        ]

    def swap(n, src, dst, rows):
        return [
            pltpu.make_async_remote_copy(
                src_ref=src.at[2 * (1 - y) + e],
                dst_ref=dst.at[pl.ds(pl.multiple_of(2 * e * rows + y * rows, rows), rows), :],
                send_sem=swap_send.at[n, e], recv_sem=swap_recv.at[n, e], device_id=across, device_id_type=MESH,
            )
            for e in range(2)
        ]

    moved = ((dec_input, x_in, 64), (memory, mem, 128), (out_grad, og, 64))
    owns = [own_rows(n, *m) for n, m in enumerate(moved)]
    swaps = [swap(n, *m) for n, m in enumerate(moved)]
    for own in owns:
        for copy in own:
            copy.start()
    greet(at)
    for n in (0, 1, 2):
        for copy in swaps[n]:
            copy.start()

    def arrived(n):
        for copy in owns[n]:
            copy.wait()
        for copy in swaps[n]:
            copy.wait_recv()

    scale = 1.0 / math.sqrt(HEAD_DIM)

    arrived(0)
    norm_forward(lambda rows: x_in[rows, :].astype(F32), first, norm_gain, norm_bias, 0)
    loads[0].wait()

    def project_qkv(n, carry):
        cols = pl.ds(pl.multiple_of(256 * n, 256), 256)
        out = jnp.dot(first[...], w_qkv[:, cols], preferred_element_type=F32)
        out = (out.astype(BF16) * jnp.where(n < 3, scale, 1.0).astype(BF16)).astype(BF16)
        qkv[2 * n] = out[:, 0:LANES]
        qkv[2 * n + 1] = out[:, LANES:256]
        return carry

    lax.fori_loop(0, 9, project_qkv, 0)

    def pair(it):
        e = it // 6
        p = it % 6
        return e, p, pl.ds(pl.multiple_of(e * 128, 128), 128), pl.ds(pl.multiple_of(p * LANES, LANES), LANES)

    def self_forward(it, carry):
        e, p, rows, lanes = pair(it)
        q_at = lax.broadcasted_iota(jnp.int32, (256, 128), 0) % 128
        k_at = lax.broadcasted_iota(jnp.int32, (256, 128), 1)
        weights, context = attend(qkv[p, rows, :], qkv[6 + p, rows, :], qkv[12 + p, rows, :], q_at >= k_at)
        p_self[it] = weights
        ctx_self[rows, lanes] = context
        return carry

    lax.fori_loop(0, 12, self_forward, 0)

    loads[1].wait()
    for n in range(3):
        cols = slice(256 * n, 256 * n + 256)
        hidden1[:, cols] = x_in[:, cols].astype(F32) + jnp.dot(ctx_self[...], w_self[:, cols], preferred_element_type=F32)
    norm_forward(lambda rows: hidden1[rows, :], second, norm_gain, norm_bias, 1)

    loads[3].wait()
    for n in range(3):
        out = jnp.dot(second[...], w_query[:, 256 * n : 256 * n + 256], preferred_element_type=F32)
        out = (out.astype(BF16) * jnp.asarray(scale, BF16)).astype(BF16)
        qx[2 * n] = out[:, 0:LANES]
        qx[2 * n + 1] = out[:, LANES:256]
    loads[2].wait()
    arrived(1)

    def project_kv(n, carry):
        cols = pl.ds(pl.multiple_of(256 * n, 256), 256)
        for e in range(2):
            out = jnp.dot(mem[256 * e : 256 * e + 256, :], w_kv[:, cols], preferred_element_type=F32).astype(BF16)
            kv[2 * n, 256 * e : 256 * e + 256, :] = out[:, 0:LANES]
            kv[2 * n + 1, 256 * e : 256 * e + 256, :] = out[:, LANES:256]
        return carry

    lax.fori_loop(0, 6, project_kv, 0)

    def cross_rows(e):
        return pl.ds(pl.multiple_of(e * 256, 256), 256)

    def cross_forward(it, carry):
        e, p, rows, lanes = pair(it)
        allowed = lax.broadcasted_iota(jnp.int32, (256, 256), 1) < src_len[2 * y + e]
        weights, context = attend(qx[p, rows, :], kv[p, cross_rows(e), :], kv[6 + p, cross_rows(e), :], allowed)
        p_cross[it] = weights
        ctx_cross[rows, lanes] = context
        return carry

    lax.fori_loop(0, 12, cross_forward, 0)

    loads[4].wait()
    for n in range(3):
        cols = slice(256 * n, 256 * n + 256)
        hidden2[:, cols] = hidden1[:, cols] + jnp.dot(ctx_cross[...], w_cross[:, cols], preferred_element_type=F32)
    norm_forward(lambda rows: hidden2[rows, :], third, norm_gain, norm_bias, 2)

    arrived(2)
    acc[...] = jnp.zeros_like(acc)
    dthird[...] = jnp.zeros_like(dthird)
    root = math.sqrt(2.0 / math.pi)

    def feed(q, carry):
        slot = q % 2

        @pl.when(q < 3)
        def _():
            for load in ffn_load(q + 1):
                load.start()

        for load in ffn_load(q):
            load.wait()
        h = q // 2
        for s in range(3):
            cols = slice(256 * s, 256 * s + 256)
            up = jnp.dot(third[...], w_in[slot, :, cols], preferred_element_type=F32)
            dact = dot(og[...], w_out[slot, cols, :], LAST)
            square = up * up
            bend = jnp.tanh(root * up * (1.0 + 0.044715 * square))
            lift = 0.5 * (1.0 + bend)
            active[:, cols] = (up * lift).astype(BF16)
            slope = lift + 0.5 * up * (1.0 - bend * bend) * (root * (1.0 + 3.0 * 0.044715 * square))
            grad = (dact * slope).astype(BF16)
            dup[:, cols] = grad
            for t in range(2):
                tile = 2 * s + t
                rg[column(4 + (q % 2) * 2 + tile // 3, h, tile % 3)] = grad[:, LANES * t : LANES * t + LANES]
        for s in range(3):
            cols = slice(256 * s, 256 * s + 256)
            acc[:, cols] += jnp.dot(active[...], w_out[slot, :, cols], preferred_element_type=F32)
            dthird[:, cols] += dot(dup[...], w_in[slot, cols, :], LAST)
        flipped = active[...].T
        for i in range(4):
            for k in range(4):
                rows = pl.ds(pl.multiple_of(48 * (2 * q + i // 2), 48), 48)
                lt[k, i % 2, rows, :] = flipped[192 * i + 48 * k : 192 * i + 48 * k + 48, :]
        return carry

    lax.fori_loop(0, 4, feed, 0)

    for k in range(4):
        for g in range(3):
            for h in range(2):
                lane = h * 384 + g * LANES
                rg[k, :, 256 * g + LANES * h : 256 * g + LANES * h + LANES] = og[:, lane : lane + LANES]
    store_left(lt, 4, third[...].T)

    def give(n, buf, out, rows, e):
        def part(which):
            return buf.at[pl.ds(pl.multiple_of(2 * e * rows + which * rows, rows), rows), :]

        stay = pltpu.make_async_copy(part(y), out.at[2 * y + e], out_sem.at[n, e])
        leave = pltpu.make_async_remote_copy(
            src_ref=part(1 - y), dst_ref=out.at[2 * y + e], send_sem=out_send.at[n, e], recv_sem=out_recv.at[n, e],
            device_id=across, device_id_type=MESH,
        )
        return stay, leave

    gives = []

    def send(n, buf, out, rows):
        for e in range(2):
            stay, leave = give(n, buf, out, rows, e)
            stay.start()
            leave.start()
            gives.append((stay, leave))

    third[...] = (hidden2[...] + acc[...]).astype(BF16)
    send(0, third, o_layer, 64)

    sums = n_own.at[0]
    sums[...] = jnp.zeros(sums.shape, F32)

    def store_grad(rows, value):
        acc[rows, :] = value

    def spread(slot):
        for g in range(3):
            for h in range(2):
                lane = h * 384 + g * LANES
                rg[slot, :, 256 * g + LANES * h : 256 * g + LANES * h + LANES] = acc[:, lane : lane + LANES].astype(BF16)

    norm_backward(
        lambda rows: hidden2[rows, :], lambda rows: dthird[rows, :],
        lambda rows, v: store_grad(rows, og[rows, :].astype(F32) + v), norm_gain, sums, 2,
    )
    spread(8)
    store_left(lt, 5, ctx_cross[...].T)

    dc = active

    def context_grad(slot, weight):
        for n in range(3):
            total = None
            for g in range(3):
                lane = g * LANES
                rows = slice(256 * n, 256 * n + 256)
                w = jnp.concatenate([weight[rows, lane : lane + LANES], weight[rows, 384 + lane : 384 + lane + LANES]], axis=1)
                term = dot(rg[slot, :, 256 * g : 256 * g + 256], w, LAST)
                total = term if total is None else total + term
            dc[:, 256 * n : 256 * n + 256] = total.astype(BF16)

    context_grad(8, w_cross)

    def cross_backward(it):
        e, p, rows, lanes = pair(it)
        dq, dk, dv = attend_back(qx[p, rows, :], kv[p, cross_rows(e), :], kv[6 + p, cross_rows(e), :], p_cross[it], dc[rows, lanes])
        h, j, g = p // 3, p // 3, p % 3
        rg[11, rows, pl.ds(pl.multiple_of(256 * g + LANES * h, LANES), LANES)] = dq
        rg[column(9 + 7 * e + j, 0, g)] = dk
        rg[column(9 + 7 * e + j, 1, g)] = dv

    def cross_loop(it, carry):
        cross_backward(it)
        return carry

    lax.fori_loop(0, 12, cross_loop, 0)

    store_left(lt, 6, mem[0:256, :].T)
    store_left(lt, 7, mem[256:512, :].T)
    for e in range(2):
        for n in range(3):
            rows = slice(256 * n, 256 * n + 256)
            mem[256 * e : 256 * e + 256, rows] = back(rg, (9 + 7 * e, 10 + 7 * e), w_kv.at[rows, :]).astype(BF16)
    send(1, mem, o_memory, 128)
    for n in range(3):
        rows = slice(256 * n, 256 * n + 256)
        dthird[:, rows] = back(rg, (11,), w_query.at[rows, :])
    norm_backward(
        lambda rows: hidden1[rows, :], lambda rows: dthird[rows, :],
        lambda rows, v: store_grad(rows, acc[rows, :] + v), norm_gain, sums, 1,
    )
    spread(12)
    context_grad(12, w_self)
    store_left(lt, 8, second[...].T)
    store_left(lt, 9, ctx_self[...].T)
    store_left(lt, 10, first[...].T)

    def self_backward(it):
        e, p, rows, lanes = pair(it)
        dq, dk, dv = attend_back(qkv[p, rows, :], qkv[6 + p, rows, :], qkv[12 + p, rows, :], p_self[it], dc[rows, lanes])
        for n, value in enumerate((dq, dk, dv)):
            tile = 6 * n + p
            h = tile // 9
            j = (tile % 9) // 3
            rg[13 + j, rows, pl.ds(pl.multiple_of(256 * (tile % 3) + LANES * h, LANES), LANES)] = value

    def self_loop(it, carry):
        self_backward(it)
        return carry

    lax.fori_loop(0, 12, self_loop, 0)

    for n in range(3):
        rows = slice(256 * n, 256 * n + 256)
        dthird[:, rows] = back(rg, (13, 14, 15), w_qkv.at[rows, :])

    def store_input(rows, v):
        x_in[rows, :] = (acc[rows, :] + v).astype(BF16)

    norm_backward(
        lambda rows: x_in[rows, :].astype(F32), lambda rows: dthird[rows, :], store_input, norm_gain, sums, 0
    )
    send(2, x_in, o_input, 64)

    def body(n, carry):
        red.tick(n)
        for j in range(6):
            @pl.when(n == 2 * j)
            def _():
                norm_step(j, at, n_own, n_got, n_send, n_recv)
        return carry

    lax.fori_loop(0, TRIPLES + 5, body, 0)
    norm_out[...] = n_own[5]
    red.drain()
    for n in range(3):
        for copy in swaps[n]:
            copy.wait_send()
    for stay, leave in gives:
        stay.wait()
        leave.wait()


def layer_call(args):
    anywhere = pl.BlockSpec(memory_space=pl.ANY)
    vmem = pl.BlockSpec(memory_space=pltpu.VMEM)
    rows = lambda width, kind=BF16: pltpu.VMEM((256, width), kind)
    return pl.pallas_call(
        layer_kernel,
        out_shape=(
            jax.ShapeDtypeStruct((4, 64, 768), BF16),
            jax.ShapeDtypeStruct((4, 64, 768), BF16),
            jax.ShapeDtypeStruct((4, 128, 768), BF16),
            jax.ShapeDtypeStruct((TRIPLES, 3, 48, 128), F32),
            jax.ShapeDtypeStruct((8, 768), F32),
        ),
        in_specs=[anywhere, anywhere, pl.BlockSpec(memory_space=pltpu.SMEM)] + [anywhere] * 8 + [vmem] * 2,
        out_specs=(anywhere, anywhere, anywhere, vmem, vmem),
        scratch_shapes=[
            rows(768), pltpu.VMEM((512, 768), BF16), rows(768),
            pltpu.VMEM((768, 2304), BF16), pltpu.VMEM((768, 768), BF16), pltpu.VMEM((768, 768), BF16),
            pltpu.VMEM((768, 1536), BF16), pltpu.VMEM((768, 768), BF16),
            pltpu.VMEM((2, 768, 768), BF16), pltpu.VMEM((2, 768, 768), BF16),
            rows(768), pltpu.VMEM((18, 256, 128), BF16), pltpu.VMEM((12, 256, 128), BF16), rows(768),
            rows(768, F32), rows(768), pltpu.VMEM((6, 256, 128), BF16), pltpu.VMEM((12, 512, 128), BF16),
            pltpu.VMEM((12, 256, 256), BF16), rows(768), rows(768, F32), rows(768),
            rows(768), rows(768), rows(768, F32), rows(768, F32),
            pltpu.VMEM((11, 2, 384, 256), BF16),
            pltpu.VMEM((18, 256, 768), BF16),
            pltpu.VMEM((6, 8, 768), F32),
            pltpu.VMEM((5, 8, 768), F32),
            pltpu.SemaphoreType.DMA((5,)),
            pltpu.SemaphoreType.DMA((5,)),
            pltpu.SemaphoreType.DMA((17,)),
            pltpu.SemaphoreType.DMA((3, 2)),
            pltpu.SemaphoreType.DMA((3, 2)),
            pltpu.SemaphoreType.DMA((3, 2)),
            pltpu.SemaphoreType.DMA((3, 2)),
            pltpu.SemaphoreType.DMA((3, 2)),
        ] + Reducer.SCRATCH,
        compiler_params=pltpu.CompilerParams(collective_id=0, has_side_effects=True, vmem_limit_bytes=60 << 20),
    )(*args)


def per_device_paired(*args):
    layer_out, input_grad, memory_grad, units, norms = layer_call(args)
    grads = gather_outputs(units)
    return (
        layer_out,
        input_grad.astype(F32),
        memory_grad.astype(F32),
        grads["self_qkv"],
        grads["self_out"],
        grads["cross_query"],
        grads["cross_kv"],
        grads["cross_out"],
        grads["ffn_in"],
        grads["ffn_out"],
        norms[0:3],
        norms[3:6],
    )

def layer_norm(x, gain, shift):
    center = jnp.mean(x, axis=-1, keepdims=True)
    centered = x - center
    spread = jnp.mean(centered * centered, axis=-1, keepdims=True)
    return centered * lax.rsqrt(spread + 1e-05) * gain + shift


def smooth(v):
    return jax.nn.gelu(v, approximate=True)


def project(rows, weight):
    return jnp.einsum("etd,df->etf", rows, weight, preferred_element_type=jnp.float32)


def project_back(grads, weight):
    return jnp.einsum("etf,df->etd", grads, weight, preferred_element_type=jnp.float32)


def outer(rows, grads):
    return jnp.einsum("etd,etf->df", rows, grads, preferred_element_type=jnp.float32)


def outer_full(rows, grads):
    return jnp.einsum(
        "etd,etf->df", rows.astype(jnp.float32), grads, precision=lax.Precision.HIGHEST
    )


def back_full(grads, weight):
    return jnp.einsum(
        "etf,df->etd", grads, weight.astype(jnp.float32), precision=lax.Precision.HIGHEST
    )


def split_heads(queries, key_values):
    examples, rows, width = queries.shape
    count = key_values.shape[1]
    heads_q = queries.reshape(examples, rows, HEADS, HEAD_DIM)
    heads_k = key_values[:, :, :width].reshape(examples, count, HEADS, HEAD_DIM)
    heads_v = key_values[:, :, width:].reshape(examples, count, HEADS, HEAD_DIM)
    return (heads_q, heads_k, heads_v)


def masked_logits(heads_q, heads_k, allowed):
    scores = jnp.einsum("eqhd,ekhd->ehqk", heads_q, heads_k, preferred_element_type=jnp.float32)
    return jnp.where(allowed, scores * (1.0 / math.sqrt(HEAD_DIM)), -1e30)


def attend_forward(queries, key_values, allowed):
    examples, rows, width = queries.shape
    heads_q, heads_k, heads_v = split_heads(queries, key_values)
    logits = masked_logits(heads_q, heads_k, allowed)
    row_top = jnp.max(logits, axis=-1, keepdims=True)
    raised = jnp.where(allowed, jnp.exp(logits - row_top), 0.0)
    row_total = jnp.sum(raised, axis=-1, keepdims=True)
    weights = (raised / row_total).astype(jnp.bfloat16)
    context = jnp.einsum("ehqk,ekhd->eqhd", weights, heads_v, preferred_element_type=jnp.float32)
    return (
        context.reshape(examples, rows, width).astype(jnp.bfloat16),
        row_top + jnp.log(row_total),
    )


def attend_backward(queries, key_values, allowed, log_total, grad_context):
    examples, rows, width = queries.shape
    count = key_values.shape[1]
    heads_q, heads_k, heads_v = split_heads(queries, key_values)
    logits = masked_logits(heads_q, heads_k, allowed)
    soft = jnp.where(allowed, jnp.exp(logits - log_total), 0.0)
    grad_heads = grad_context.reshape(examples, rows, HEADS, HEAD_DIM)
    grad_soft = jnp.einsum(
        "eqhd,ekhd->ehqk", grad_heads, heads_v, preferred_element_type=jnp.float32
    )
    grad_values = jnp.einsum(
        "ehqk,eqhd->ekhd", soft.astype(jnp.bfloat16), grad_heads, preferred_element_type=jnp.float32
    )
    inner = jnp.sum(soft * grad_soft, axis=-1, keepdims=True)
    grad_scores = (soft * (grad_soft - inner) * (1.0 / math.sqrt(HEAD_DIM))).astype(jnp.bfloat16)
    grad_queries = jnp.einsum(
        "ehqk,ekhd->eqhd", grad_scores, heads_k, preferred_element_type=jnp.float32
    )
    grad_keys = jnp.einsum(
        "ehqk,eqhd->ekhd", grad_scores, heads_q, preferred_element_type=jnp.float32
    )
    joined = jnp.concatenate(
        [grad_keys.reshape(examples, count, width), grad_values.reshape(examples, count, width)],
        axis=2,
    )
    return (grad_queries.reshape(examples, rows, width), joined)


def per_device_wide(
    dec_input,
    memory,
    src_len,
    out_grad,
    self_qkv,
    self_out,
    cross_query,
    cross_kv,
    cross_out,
    ffn_in,
    ffn_out,
    norm_gain,
    norm_bias,
):
    examples, local_rows, width = dec_input.shape
    local_sources = memory.shape[1]
    seq_count = lax.axis_size("seq")
    all_targets = local_rows * seq_count
    all_sources = local_sources * seq_count
    rank = lax.axis_index("seq")
    x = dec_input.astype(jnp.float32)
    first_f, pull_first = jax.vjp(layer_norm, x, norm_gain[0], norm_bias[0])
    first = first_f.astype(jnp.bfloat16)
    projected = project(first, self_qkv).astype(jnp.bfloat16)
    self_queries = projected[:, :, :width]
    self_kv = lax.all_gather(projected[:, :, width:], "seq", axis=1, tiled=True)
    query_place = rank * local_rows + jnp.arange(local_rows, dtype=jnp.int32)
    key_place = jnp.arange(all_targets, dtype=jnp.int32)
    causal = (query_place[:, None] >= key_place[None, :])[None, None]
    self_context, self_total = attend_forward(self_queries, self_kv, causal)
    hidden1 = x + project(self_context, self_out)
    second_f, pull_second = jax.vjp(layer_norm, hidden1, norm_gain[1], norm_bias[1])
    second = second_f.astype(jnp.bfloat16)
    cross_queries = project(second, cross_query).astype(jnp.bfloat16)
    gathered = lax.all_gather(memory, "seq", axis=1, tiled=True)
    memory_kv = project(gathered, cross_kv).astype(jnp.bfloat16)
    source_place = jnp.arange(all_sources, dtype=jnp.int32)
    visible = (source_place[None, :] < src_len[:, None])[:, None, None, :]
    cross_context, cross_total = attend_forward(cross_queries, memory_kv, visible)
    hidden2 = hidden1 + project(cross_context, cross_out)
    third_f, pull_third = jax.vjp(layer_norm, hidden2, norm_gain[2], norm_bias[2])
    third = third_f.astype(jnp.bfloat16)
    raised_up = project(third, ffn_in)
    active_f, pull_smooth = jax.vjp(smooth, raised_up)
    activated = active_f.astype(jnp.bfloat16)
    layer_out = (hidden2 + project(activated, ffn_out)).astype(jnp.bfloat16)
    grad_out = out_grad.astype(jnp.float32)
    ffn_out_grad = outer(activated, out_grad)
    (grad_up,) = pull_smooth(project_back(out_grad, ffn_out))
    grad_up_low = grad_up.astype(jnp.bfloat16)
    ffn_in_grad = outer(third, grad_up_low)
    back_third, gain_third, bias_third = pull_third(project_back(grad_up_low, ffn_in))
    grad_hidden2 = grad_out + back_third
    cross_branch = grad_hidden2.astype(jnp.bfloat16)
    cross_out_grad = outer(cross_context, cross_branch)
    grad_cross_context = project_back(cross_branch, cross_out).astype(jnp.bfloat16)
    grad_cross_q, grad_memory_kv = attend_backward(
        cross_queries, memory_kv, visible, cross_total, grad_cross_context
    )
    local_kv_grad = lax.psum_scatter(
        grad_memory_kv.astype(jnp.bfloat16), "seq", scatter_dimension=1, tiled=True
    ).astype(jnp.float32)
    cross_kv_grad = outer_full(memory, local_kv_grad)
    memory_grad = back_full(local_kv_grad, cross_kv)
    grad_cross_low = grad_cross_q.astype(jnp.bfloat16)
    cross_query_grad = outer(second, grad_cross_low)
    back_second, gain_second, bias_second = pull_second(project_back(grad_cross_low, cross_query))
    grad_hidden1 = grad_hidden2 + back_second
    self_branch = grad_hidden1.astype(jnp.bfloat16)
    self_out_grad = outer(self_context, self_branch)
    grad_self_context = project_back(self_branch, self_out).astype(jnp.bfloat16)
    grad_self_q, grad_self_kv = attend_backward(
        self_queries, self_kv, causal, self_total, grad_self_context
    )
    local_self_kv = lax.psum_scatter(grad_self_kv, "seq", scatter_dimension=1, tiled=True)
    grad_projected = jnp.concatenate([grad_self_q, local_self_kv], axis=2).astype(jnp.bfloat16)
    self_qkv_grad = outer(first, grad_projected)
    back_first, gain_first, bias_first = pull_first(project_back(grad_projected, self_qkv))
    input_grad = grad_hidden1 + back_first
    gain_terms = jnp.stack([gain_first, gain_second, gain_third])
    bias_terms = jnp.stack([bias_first, bias_second, bias_third])
    gain_total, bias_total = lax.psum((gain_terms, bias_terms), ("dp", "seq"))
    partial_value = (
        lax.psum_scatter(
            self_qkv_grad.astype(jnp.bfloat16), "dp", scatter_dimension=0, tiled=True
        ).astype(jnp.float32),
        lax.psum_scatter(
            self_out_grad.astype(jnp.bfloat16), "dp", scatter_dimension=0, tiled=True
        ).astype(jnp.float32),
        lax.psum_scatter(
            cross_query_grad.astype(jnp.bfloat16), "dp", scatter_dimension=0, tiled=True
        ).astype(jnp.float32),
        lax.psum_scatter(
            cross_kv_grad.astype(jnp.bfloat16), "dp", scatter_dimension=0, tiled=True
        ).astype(jnp.float32),
        lax.psum_scatter(
            cross_out_grad.astype(jnp.bfloat16), "dp", scatter_dimension=0, tiled=True
        ).astype(jnp.float32),
        lax.psum_scatter(
            ffn_in_grad.astype(jnp.bfloat16), "dp", scatter_dimension=0, tiled=True
        ).astype(jnp.float32),
        lax.psum_scatter(
            ffn_out_grad.astype(jnp.bfloat16), "dp", scatter_dimension=0, tiled=True
        ).astype(jnp.float32),
    )
    finished = (
        lax.psum_scatter(
            partial_value[0].astype(jnp.bfloat16), "seq", scatter_dimension=1, tiled=True
        ).astype(jnp.float32),
        lax.psum_scatter(
            partial_value[1].astype(jnp.bfloat16), "seq", scatter_dimension=1, tiled=True
        ).astype(jnp.float32),
        lax.psum_scatter(
            partial_value[2].astype(jnp.bfloat16), "seq", scatter_dimension=1, tiled=True
        ).astype(jnp.float32),
        lax.psum_scatter(
            partial_value[3].astype(jnp.bfloat16), "seq", scatter_dimension=1, tiled=True
        ).astype(jnp.float32),
        lax.psum_scatter(
            partial_value[4].astype(jnp.bfloat16), "seq", scatter_dimension=1, tiled=True
        ).astype(jnp.float32),
        lax.psum_scatter(
            partial_value[5].astype(jnp.bfloat16), "seq", scatter_dimension=1, tiled=True
        ).astype(jnp.float32),
        lax.psum_scatter(
            partial_value[6].astype(jnp.bfloat16), "seq", scatter_dimension=1, tiled=True
        ).astype(jnp.float32),
    )
    return (
        layer_out,
        input_grad,
        memory_grad,
        finished[0],
        finished[1],
        finished[2],
        finished[3],
        finished[4],
        finished[5],
        finished[6],
        gain_total,
        bias_total,
    )


def solution(mesh):
    paired = mesh.shape["dp"] == 16 and mesh.shape["seq"] == 2
    per_device = per_device_paired if paired else per_device_wide
    in_specs = (
        P("dp", "seq", None),
        P("dp", "seq", None),
        P("dp"),
        P("dp", "seq", None),
        P(),
        P(),
        P(),
        P(),
        P(),
        P(),
        P(),
        P(),
        P(),
    )
    out_specs = (
        P("dp", "seq", None),
        P("dp", "seq", None),
        P("dp", "seq", None),
        P("dp", "seq"),
        P("dp", "seq"),
        P("dp", "seq"),
        P("dp", "seq"),
        P("dp", "seq"),
        P("dp", "seq"),
        P("dp", "seq"),
        P(),
        P(),
    )
    return jax.shard_map(
        per_device, mesh=mesh, in_specs=in_specs, out_specs=out_specs, check_vma=False
    )
```

profile of v0, /device:TPU:0, one launch (start us, length us, event | category | flops | bytes accessed | tf_op | source)
XLA Modules:
  0.0 157.7 jit_solution(17927805457030915809)
XLA Ops:
  0.6 147.0 %shard_map.220 = (bf16[4,64,768]{2,1,0:T(8,128)(2,1)}, bf16[4,64,768]{2,1,0:T(8,128)(2,1)}, bf16[4,128,768]{2,1,0:T(8,128)(2,1)}, f32[16,3,48,128]{3,2,1,0:T(8,128)}, f32[8,768]{1,0:T(8,128)}) custom-call(bf16[4,64,768]{2,1,0:T(8,128)(2,1)} %dec_input.1, bf16[4,128,768]{2,1,0:T(8,128)(2,1)} %memory.1, s32[4]{0:T(128)} %src_len.1, ...), custom_call_target="tpu_custom_call" | custom-call | tf_op jit(solution)/shard_map/pallas_call | solution.py:641
  147.7 0.0 copy-start
  147.7 1.1 slice_bitcast_fusion.4
  148.8 0.7 copy_bitcast_fusion.1
  149.5 0.6 copy.41
  150.2 0.0 copy-done
  150.2 0.2 copy.31
  150.4 0.7 copy.40
  151.1 0.2 copy.30
  151.3 0.9 reshape.50
  152.2 0.0 copy-start.4
  152.2 0.0 copy-start.1
  152.2 0.1 copy.25
  152.3 0.8 reshape.45
  153.1 0.1 copy.28
  153.2 0.7 reshape.48
  153.9 0.0 copy-done.4
  153.9 0.6 fusion
  154.6 0.0 copy-done.1
  154.6 0.0 copy-start.3
  154.6 1.3 convert_element_type.7
  155.8 0.0 copy-start.2
  155.8 0.0 copy-done.3
  155.8 0.9 convert_element_type.6
  156.8 0.1 copy-done.2
  156.9 0.7 copy.43
  (6 shorter events, 0.2 us)
Async XLA Ops:
  147.7 2.5 %copy-start = (f32[16,3,48,128]{3,2,1,0:T(8,128)S(1)}, f32[16,3,48,128]{3,2,1,0:T(8,128)}, u32[]{:S(2)}) copy-start(f32[16,3,48,128]{3,2,1,0:T(8,128)} %get-tuple-element.20) | copy-start | bytes 3538948
  152.2 1.8 %copy-start.4 = (f32[8,768]{1,0:T(8,128)S(1)}, f32[8,768]{1,0:T(8,128)}, u32[]{:S(2)}) copy-start(f32[8,768]{1,0:T(8,128)} %get-tuple-element.21) | copy-start | bytes 73732
  152.2 2.4 %copy-start.1 = (bf16[4,128,768]{2,1,0:T(8,128)(2,1)S(1)}, bf16[4,128,768]{2,1,0:T(8,128)(2,1)}, u32[]{:S(2)}) copy-start(bf16[4,128,768]{2,1,0:T(8,128)(2,1)} %get-tuple-element.19) | copy-start | bytes 2359300
  154.6 1.3 copy-start.3
  155.8 1.1 copy-start.2
where the time goes:
time: 158 us
  Pallas kernels  147 us (93%)
  local copies, waits for them, and re-layouts  7.73 us (5%)
  other arithmetic  2.21 us (1%)
    pallas_call x1, Pallas kernels, layer_call(): pl.pallas_call(layer_kernel, out_shape=(jax.ShapeDtypeStruct((4, 64, 768)...  147 us

commit v1 on v0

--- a/solution.py
+++ b/solution.py
@@ -38,8 +38,28 @@
     pl.semaphore_wait(barrier, 5)
 
 
-def left_slot(t):
-    return jnp.where(t < 4, t, jnp.where(t < 8, 4, jnp.where(t == 8, 5, jnp.where(t < 11, 6, jnp.where(t == 11, 8, jnp.where(t == 12, 9, 10))))))
+LEFT = (0, 1, 2, 3, 4, 4, 4, 4, 5, 6, 6, 8, 9, 10, 10, 10)
+RIGHT = (0, 0, 0, 0, 1, 2, 3, 4, 5, 6, 7, 8, 9, 10, 11, 12)
+
+
+def look_up(table, t):
+    if isinstance(t, int):
+        return table[t]
+    value = table[-1]
+    for n in range(TRIPLES - 2, -1, -1):
+        if table[n] != table[n + 1]:
+            value = jnp.where(t <= n, table[n], value)
+    return value
+
+
+def when(condition):
+    if isinstance(condition, bool):
+        return (lambda body: body()) if condition else (lambda body: None)
+    return pl.when(condition)
+
+
+def negate(condition):
+    return not condition if isinstance(condition, bool) else jnp.logical_not(condition)
 
 
 def store_left(lt, slot, rows_by_feature):
@@ -48,24 +68,30 @@
 
 
 class Reducer:
+    LAGS = (0, 1, 3, 5, 7, 8)
+    SLOTS = (2, 3, 3, 3, 3)
+    TICKS = TRIPLES + 8
     SCRATCH = [
         pltpu.VMEM((2, 3, 384, 256), BF16),
         pltpu.VMEM((TRIPLES, 3, 384, 256), BF16),
-        pltpu.VMEM((2, 3, 2, 2, 2, 2, 48, 128), BF16),
+        pltpu.VMEM((3, 3, 2, 2, 2, 2, 48, 128), BF16),
         pltpu.VMEM((TRIPLES, 3, 2, 2, 2, 48, 128), BF16),
-        pltpu.VMEM((2, 3, 2, 2, 2, 48, 128), BF16),
+        pltpu.VMEM((3, 3, 2, 2, 2, 48, 128), BF16),
         pltpu.VMEM((TRIPLES, 3, 2, 2, 48, 128), BF16),
-        pltpu.VMEM((2, 3, 2, 2, 48, 128), BF16),
+        pltpu.VMEM((3, 3, 2, 2, 48, 128), BF16),
         pltpu.VMEM((TRIPLES, 3, 2, 48, 128), BF16),
-        pltpu.VMEM((2, 3, 2, 48, 128), BF16),
+        pltpu.VMEM((3, 3, 2, 48, 128), BF16),
         pltpu.VMEM((TRIPLES, 3, 48, 128), BF16),
-        pltpu.SemaphoreType.DMA((5, 2, 3)),
+        pltpu.VMEM((3, 3, 48, 128), F32),
+        pltpu.SemaphoreType.DMA((3,)),
+        pltpu.SemaphoreType.DMA((5, 3, 3)),
         pltpu.SemaphoreType.DMA((5, TRIPLES, 3)),
     ]
 
-    def __init__(self, at, lt, rg, out, s0, r0, s1, r1, s2, r2, s3, r3, s4, r4, send_sem, recv_sem):
+    def __init__(self, at, lt, rg, out, s0, r0, s1, r1, s2, r2, s3, r3, s4, r4, done, done_sem, send_sem, recv_sem):
         self.at, self.lt, self.rg, self.out = at, lt, rg, out
         self.sent, self.got = (s0, s1, s2, s3, s4), (r0, r1, r2, r3, r4)
+        self.done, self.done_sem = done, done_sem
         self.send_sem, self.recv_sem = send_sem, recv_sem
 
     def axis(self, stage, g):
@@ -73,7 +99,7 @@
 
     def copy(self, stage, t, g):
         axis = self.axis(stage, g)
-        slot = t % 2
+        slot = t % self.SLOTS[stage]
         src = self.sent[stage].at[slot, g]
         if stage:
             src = src.at[1 - self.at[axis]]
@@ -87,15 +113,16 @@
         )
 
     def free(self, stage, t):
-        @pl.when(t >= 2)
+        slots = self.SLOTS[stage]
+
+        @when(t >= slots)
         def _():
             for g in range(3):
-                self.copy(stage, t - 2, g).wait_send()
+                self.copy(stage, t - slots, g).wait_send()
 
     def product(self, t, half, g):
         cols = slice(256 * g, 256 * g + 256)
-        slot = left_slot(t)
-        return jnp.dot(self.lt[slot, half], self.rg[t, :, cols], preferred_element_type=F32)
+        return jnp.dot(self.lt[look_up(LEFT, t), half], self.rg[look_up(RIGHT, t), :, cols], preferred_element_type=F32)
 
     def first(self, t):
         self.free(0, t)
@@ -104,13 +131,13 @@
         for g in range(3):
             cols = slice(256 * g, 256 * g + 256)
 
-            @pl.when(jnp.logical_not(memory))
+            @when(negate(memory))
             def _():
                 self.sent[0][t % 2, g] = self.product(t, half, g).astype(BF16)
 
-            @pl.when(memory)
+            @when(memory)
             def _():
-                more = jnp.dot(self.lt[7, half], self.rg[t + 7, :, cols], preferred_element_type=F32)
+                more = jnp.dot(self.lt[7, half], self.rg[t + 4, :, cols], preferred_element_type=F32)
                 self.sent[0][t % 2, g] = (self.product(t, half, g) + more).astype(BF16)
 
             self.copy(0, t, g).start()
@@ -130,37 +157,48 @@
                     for y in range(2):
                         bits["y"] = y
                         where = tuple(bits[a] for a in order)
-                        self.sent[1][(t % 2, g) + where] = total[48 * b : 48 * b + 48, 128 * y : 128 * y + 128].astype(BF16)
-
-            @pl.when(jnp.logical_not(memory))
+                        self.sent[1][(t % self.SLOTS[1], g) + where] = total[48 * b : 48 * b + 48, 128 * y : 128 * y + 128].astype(BF16)
+
+            @when(negate(memory))
             def _():
                 spread(self.product(t, half, g) + self.got[0][t, g].astype(F32))
 
-            @pl.when(memory)
+            @when(memory)
             def _():
-                more = jnp.dot(self.lt[7, half], self.rg[t + 7, :, cols], preferred_element_type=F32)
+                more = jnp.dot(self.lt[7, half], self.rg[t + 4, :, cols], preferred_element_type=F32)
                 spread(self.product(t, half, g) + more + self.got[0][t, g].astype(F32))
 
             self.copy(1, t, g).start()
+
+    def write(self, t):
+        return pltpu.make_async_copy(self.done.at[t % 3], self.out.at[t], self.done_sem.at[t % 3])
 
     def onward(self, stage, t):
         if stage < 5:
             self.free(stage, t)
+        else:
+
+            @when(t >= 3)
+            def _():
+                self.write(t - 3).wait()
+
         for g in range(3):
             self.copy(stage - 1, t, g).wait_recv()
-            own = self.sent[stage - 1][t % 2, g, self.at[self.axis(stage - 1, g)]]
+            own = self.sent[stage - 1][t % self.SLOTS[stage - 1], g, self.at[self.axis(stage - 1, g)]]
             total = own.astype(F32) + self.got[stage - 1][t, g].astype(F32)
             if stage < 5:
-                self.sent[stage][t % 2, g] = total.astype(BF16)
+                self.sent[stage][t % self.SLOTS[stage], g] = total.astype(BF16)
                 self.copy(stage, t, g).start()
             else:
-                self.out[t, g] = total
+                self.done[t % 3, g] = total
+        if stage == 5:
+            self.write(t).start()
 
     def tick(self, n):
         for stage in range(6):
-            t = n - stage
-
-            @pl.when((t >= 0) & (t < TRIPLES))
+            t = n - self.LAGS[stage]
+
+            @when((t >= 0) & (t < TRIPLES))
             def _():
                 if stage == 0:
                     self.first(t)
@@ -170,8 +208,10 @@
                     self.onward(stage, t)
 
     def drain(self):
+        for t in range(TRIPLES - 3, TRIPLES):
+            self.write(t).wait()
         for stage in range(5):
-            for t in (TRIPLES - 2, TRIPLES - 1):
+            for t in range(TRIPLES - self.SLOTS[stage], TRIPLES):
                 for g in range(3):
                     self.copy(stage, t, g).wait_send()
 
@@ -194,17 +234,6 @@
         norm_copy(j, at, own, got, send_sem, recv_sem).start()
 
 
-def assemble(units, first, count):
-    block = units[first : first + count]
-    return jnp.transpose(block, (2, 0, 1, 3)).reshape(48, count * 384)
-
-
-def gather_outputs(units):
-    ffn_out = jnp.transpose(units[0:4], (0, 2, 1, 3)).reshape(192, 384)
-    return dict(ffn_out=ffn_out, ffn_in=assemble(units, 4, 4), cross_out=assemble(units, 8, 1), cross_kv=assemble(units, 9, 2),
-                cross_query=assemble(units, 11, 1), self_out=assemble(units, 12, 1), self_qkv=assemble(units, 13, 3))
-
-
 LANES = 128
 
 
@@ -217,11 +246,8 @@
 
 
 def row_blocks(step, body):
-    def run(b, carry):
-        body(pl.ds(pl.multiple_of(b * step, step), step))
-        return carry
-
-    lax.fori_loop(0, 256 // step, run, 0)
+    for b in range(256 // step):
+        body(slice(b * step, b * step + step))
 
 
 def norm_forward(load, out, norm_gain, norm_bias, k):
@@ -308,7 +334,7 @@
     o_layer, o_input, o_memory, units, norm_out,
     x_in, mem, og, w_qkv, w_self, w_query, w_kv, w_cross, w_in, w_out,
     first, qkv, p_self, ctx_self, hidden1, second, qx, kv, p_cross, ctx_cross, hidden2, third,
-    active, dup, acc, dthird,
+    active, acc, dthird,
     lt, rg, n_own, n_got, n_send, n_recv, load_sem, swap_send, swap_recv, out_sem, out_send, out_recv, *rest
 ):
     at = place()
@@ -361,15 +387,17 @@
         for copy in own:
             copy.start()
     greet(at)
-    for n in (0, 1, 2):
-        for copy in swaps[n]:
-            copy.start()
+    for copy in swaps[0]:
+        copy.start()
 
     def arrived(n):
         for copy in owns[n]:
             copy.wait()
         for copy in swaps[n]:
-            copy.wait_recv()
+            copy.wait()
+        if n < 2:
+            for copy in swaps[n + 1]:
+                copy.start()
 
     scale = 1.0 / math.sqrt(HEAD_DIM)
 
@@ -387,21 +415,20 @@
 
     lax.fori_loop(0, 9, project_qkv, 0)
 
-    def pair(it):
-        e = it // 6
-        p = it % 6
-        return e, p, pl.ds(pl.multiple_of(e * 128, 128), 128), pl.ds(pl.multiple_of(p * LANES, LANES), LANES)
-
-    def self_forward(it, carry):
-        e, p, rows, lanes = pair(it)
+    def pair(e, p):
+        return slice(e * 128, e * 128 + 128), pl.ds(pl.multiple_of(p * LANES, LANES), LANES)
+
+    def self_forward(p, carry):
         q_at = lax.broadcasted_iota(jnp.int32, (256, 128), 0) % 128
         k_at = lax.broadcasted_iota(jnp.int32, (256, 128), 1)
-        weights, context = attend(qkv[p, rows, :], qkv[6 + p, rows, :], qkv[12 + p, rows, :], q_at >= k_at)
-        p_self[it] = weights
-        ctx_self[rows, lanes] = context
+        for e in range(2):
+            rows, lanes = pair(e, p)
+            weights, context = attend(qkv[p, rows, :], qkv[6 + p, rows, :], qkv[12 + p, rows, :], q_at >= k_at)
+            p_self[6 * e + p] = weights
+            ctx_self[rows, lanes] = context
         return carry
 
-    lax.fori_loop(0, 12, self_forward, 0)
+    lax.fori_loop(0, 6, self_forward, 0)
 
     loads[1].wait()
     for n in range(3):
@@ -420,26 +447,26 @@
 
     def project_kv(n, carry):
         cols = pl.ds(pl.multiple_of(256 * n, 256), 256)
+        out = jnp.dot(mem[...], w_kv[:, cols], preferred_element_type=F32).astype(BF16)
+        kv[2 * n] = out[:, 0:LANES]
+        kv[2 * n + 1] = out[:, LANES:256]
+        return carry
+
+    lax.fori_loop(0, 6, project_kv, 0)
+
+    def cross_rows(e):
+        return slice(e * 256, e * 256 + 256)
+
+    def cross_forward(p, carry):
         for e in range(2):
-            out = jnp.dot(mem[256 * e : 256 * e + 256, :], w_kv[:, cols], preferred_element_type=F32).astype(BF16)
-            kv[2 * n, 256 * e : 256 * e + 256, :] = out[:, 0:LANES]
-            kv[2 * n + 1, 256 * e : 256 * e + 256, :] = out[:, LANES:256]
+            rows, lanes = pair(e, p)
+            allowed = lax.broadcasted_iota(jnp.int32, (256, 256), 1) < src_len[2 * y + e]
+            weights, context = attend(qx[p, rows, :], kv[p, cross_rows(e), :], kv[6 + p, cross_rows(e), :], allowed)
+            p_cross[6 * e + p] = weights
+            ctx_cross[rows, lanes] = context
         return carry
 
-    lax.fori_loop(0, 6, project_kv, 0)
-
-    def cross_rows(e):
-        return pl.ds(pl.multiple_of(e * 256, 256), 256)
-
-    def cross_forward(it, carry):
-        e, p, rows, lanes = pair(it)
-        allowed = lax.broadcasted_iota(jnp.int32, (256, 256), 1) < src_len[2 * y + e]
-        weights, context = attend(qx[p, rows, :], kv[p, cross_rows(e), :], kv[6 + p, cross_rows(e), :], allowed)
-        p_cross[it] = weights
-        ctx_cross[rows, lanes] = context
-        return carry
-
-    lax.fori_loop(0, 12, cross_forward, 0)
+    lax.fori_loop(0, 6, cross_forward, 0)
 
     loads[4].wait()
     for n in range(3):
@@ -448,6 +475,14 @@
     norm_forward(lambda rows: hidden2[rows, :], third, norm_gain, norm_bias, 2)
 
     arrived(2)
+
+    def spread(slot, rows_of):
+        for g in range(3):
+            for h in range(2):
+                lane = h * 384 + g * LANES
+                rg[slot, :, 256 * g + LANES * h : 256 * g + LANES * h + LANES] = rows_of[:, lane : lane + LANES].astype(BF16)
+
+    spread(0, og)
     acc[...] = jnp.zeros_like(acc)
     dthird[...] = jnp.zeros_like(dthird)
     root = math.sqrt(2.0 / math.pi)
@@ -462,7 +497,10 @@
 
         for load in ffn_load(q):
             load.wait()
-        h = q // 2
+
+        def up_tile(tile):
+            return column(1 + (q % 2) * 2 + tile // 3, q // 2, tile % 3)
+
         for s in range(3):
             cols = slice(256 * s, 256 * s + 256)
             up = jnp.dot(third[...], w_in[slot, :, cols], preferred_element_type=F32)
@@ -473,14 +511,14 @@
             active[:, cols] = (up * lift).astype(BF16)
             slope = lift + 0.5 * up * (1.0 - bend * bend) * (root * (1.0 + 3.0 * 0.044715 * square))
             grad = (dact * slope).astype(BF16)
-            dup[:, cols] = grad
             for t in range(2):
                 tile = 2 * s + t
-                rg[column(4 + (q % 2) * 2 + tile // 3, h, tile % 3)] = grad[:, LANES * t : LANES * t + LANES]
+                rg[up_tile(tile)] = grad[:, LANES * t : LANES * t + LANES]
+        dup = jnp.concatenate([rg[up_tile(tile)] for tile in range(6)], axis=1)
         for s in range(3):
             cols = slice(256 * s, 256 * s + 256)
             acc[:, cols] += jnp.dot(active[...], w_out[slot, :, cols], preferred_element_type=F32)
-            dthird[:, cols] += dot(dup[...], w_in[slot, cols, :], LAST)
+            dthird[:, cols] += dot(dup, w_in[slot, cols, :], LAST)
         flipped = active[...].T
         for i in range(4):
             for k in range(4):
@@ -490,122 +528,119 @@
 
     lax.fori_loop(0, 4, feed, 0)
 
-    for k in range(4):
-        for g in range(3):
-            for h in range(2):
-                lane = h * 384 + g * LANES
-                rg[k, :, 256 * g + LANES * h : 256 * g + LANES * h + LANES] = og[:, lane : lane + LANES]
+    PIECES = (
+        [(third, o_layer, 64, e, r) for e in range(2) for r in (0, 32)]
+        + [(mem, o_memory, 128, e, r) for e in range(2) for r in (0, 32, 64, 96)]
+        + [(x_in, o_input, 64, e, r) for e in range(2) for r in (0, 32)]
+    )
+
+    def piece(n, leaving):
+        buf, out, rows, e, r = PIECES[n]
+        which = 1 - y if leaving else y
+        src = buf.at[pl.ds(pl.multiple_of(2 * e * rows + which * rows + r, 32), 32), :]
+        dst = out.at[2 * y + e, r : r + 32, :]
+        if not leaving:
+            return pltpu.make_async_copy(src, dst, out_sem.at[n])
+        return pltpu.make_async_remote_copy(
+            src_ref=src, dst_ref=dst, send_sem=out_send.at[n], recv_sem=out_recv.at[n], device_id=across, device_id_type=MESH
+        )
+
+    def send(n):
+        piece(n, True).start()
+        piece(n, False).start()
+
+    def tick(n):
+        red.tick(n)
+        if n:
+            send(n - 1)
+
+    tick(0)
     store_left(lt, 4, third[...].T)
 
-    def give(n, buf, out, rows, e):
-        def part(which):
-            return buf.at[pl.ds(pl.multiple_of(2 * e * rows + which * rows, rows), rows), :]
-
-        stay = pltpu.make_async_copy(part(y), out.at[2 * y + e], out_sem.at[n, e])
-        leave = pltpu.make_async_remote_copy(
-            src_ref=part(1 - y), dst_ref=out.at[2 * y + e], send_sem=out_send.at[n, e], recv_sem=out_recv.at[n, e],
-            device_id=across, device_id_type=MESH,
-        )
-        return stay, leave
-
-    gives = []
-
-    def send(n, buf, out, rows):
-        for e in range(2):
-            stay, leave = give(n, buf, out, rows, e)
-            stay.start()
-            leave.start()
-            gives.append((stay, leave))
-
     third[...] = (hidden2[...] + acc[...]).astype(BF16)
-    send(0, third, o_layer, 64)
 
     sums = n_own.at[0]
     sums[...] = jnp.zeros(sums.shape, F32)
 
     def store_grad(rows, value):
         acc[rows, :] = value
-
-    def spread(slot):
-        for g in range(3):
-            for h in range(2):
-                lane = h * 384 + g * LANES
-                rg[slot, :, 256 * g + LANES * h : 256 * g + LANES * h + LANES] = acc[:, lane : lane + LANES].astype(BF16)
 
     norm_backward(
         lambda rows: hidden2[rows, :], lambda rows: dthird[rows, :],
         lambda rows, v: store_grad(rows, og[rows, :].astype(F32) + v), norm_gain, sums, 2,
     )
-    spread(8)
+    spread(5, acc)
+    tick(1)
     store_left(lt, 5, ctx_cross[...].T)
-
     dc = active
 
     def context_grad(slot, weight):
         for n in range(3):
-            total = None
-            for g in range(3):
-                lane = g * LANES
-                rows = slice(256 * n, 256 * n + 256)
-                w = jnp.concatenate([weight[rows, lane : lane + LANES], weight[rows, 384 + lane : 384 + lane + LANES]], axis=1)
-                term = dot(rg[slot, :, 256 * g : 256 * g + 256], w, LAST)
-                total = term if total is None else total + term
-            dc[:, 256 * n : 256 * n + 256] = total.astype(BF16)
-
-    context_grad(8, w_cross)
-
-    def cross_backward(it):
-        e, p, rows, lanes = pair(it)
-        dq, dk, dv = attend_back(qx[p, rows, :], kv[p, cross_rows(e), :], kv[6 + p, cross_rows(e), :], p_cross[it], dc[rows, lanes])
-        h, j, g = p // 3, p // 3, p % 3
-        rg[11, rows, pl.ds(pl.multiple_of(256 * g + LANES * h, LANES), LANES)] = dq
-        rg[column(9 + 7 * e + j, 0, g)] = dk
-        rg[column(9 + 7 * e + j, 1, g)] = dv
-
-    def cross_loop(it, carry):
-        cross_backward(it)
+            rows = slice(256 * n, 256 * n + 256)
+            dc[:, rows] = back(rg, (slot,), weight.at[rows, :]).astype(BF16)
+
+    context_grad(5, w_cross)
+
+    def cross_backward(p, carry):
+        for e in range(2):
+            rows, lanes = pair(e, p)
+            dq, dk, dv = attend_back(qx[p, rows, :], kv[p, cross_rows(e), :], kv[6 + p, cross_rows(e), :], p_cross[6 * e + p], dc[rows, lanes])
+            h, j, g = p // 3, p // 3, p % 3
+            rg[8, rows, pl.ds(pl.multiple_of(256 * g + LANES * h, LANES), LANES)] = dq
+            rg[column(6 + 7 * e + j, 0, g)] = dk
+            rg[column(6 + 7 * e + j, 1, g)] = dv
         return carry
 
-    lax.fori_loop(0, 12, cross_loop, 0)
+    tick(2)
+    lax.fori_loop(0, 3, cross_backward, 0)
+    tick(3)
+    lax.fori_loop(3, 6, cross_backward, 0)
 
     store_left(lt, 6, mem[0:256, :].T)
     store_left(lt, 7, mem[256:512, :].T)
-    for e in range(2):
+
+    def memory_rows(e):
         for n in range(3):
             rows = slice(256 * n, 256 * n + 256)
-            mem[256 * e : 256 * e + 256, rows] = back(rg, (9 + 7 * e, 10 + 7 * e), w_kv.at[rows, :]).astype(BF16)
-    send(1, mem, o_memory, 128)
+            mem[256 * e : 256 * e + 256, rows] = back(rg, (6 + 7 * e, 7 + 7 * e), w_kv.at[rows, :]).astype(BF16)
+
+    memory_rows(0)
+    tick(4)
+    memory_rows(1)
     for n in range(3):
         rows = slice(256 * n, 256 * n + 256)
-        dthird[:, rows] = back(rg, (11,), w_query.at[rows, :])
+        dthird[:, rows] = back(rg, (8,), w_query.at[rows, :])
+    tick(5)
     norm_backward(
         lambda rows: hidden1[rows, :], lambda rows: dthird[rows, :],
         lambda rows, v: store_grad(rows, acc[rows, :] + v), norm_gain, sums, 1,
     )
-    spread(12)
-    context_grad(12, w_self)
+    spread(9, acc)
+    context_grad(9, w_self)
+    tick(6)
     store_left(lt, 8, second[...].T)
     store_left(lt, 9, ctx_self[...].T)
     store_left(lt, 10, first[...].T)
 
-    def self_backward(it):
-        e, p, rows, lanes = pair(it)
-        dq, dk, dv = attend_back(qkv[p, rows, :], qkv[6 + p, rows, :], qkv[12 + p, rows, :], p_self[it], dc[rows, lanes])
-        for n, value in enumerate((dq, dk, dv)):
-            tile = 6 * n + p
-            h = tile // 9
-            j = (tile % 9) // 3
-            rg[13 + j, rows, pl.ds(pl.multiple_of(256 * (tile % 3) + LANES * h, LANES), LANES)] = value
-
-    def self_loop(it, carry):
-        self_backward(it)
+    def self_backward(p, carry):
+        for e in range(2):
+            rows, lanes = pair(e, p)
+            dq, dk, dv = attend_back(qkv[p, rows, :], qkv[6 + p, rows, :], qkv[12 + p, rows, :], p_self[6 * e + p], dc[rows, lanes])
+            for n, value in enumerate((dq, dk, dv)):
+                tile = 6 * n + p
+                h = tile // 9
+                j = (tile % 9) // 3
+                rg[10 + j, rows, pl.ds(pl.multiple_of(256 * (tile % 3) + LANES * h, LANES), LANES)] = value
         return carry
 
-    lax.fori_loop(0, 12, self_loop, 0)
-
+    lax.fori_loop(0, 3, self_backward, 0)
+    tick(7)
+    lax.fori_loop(3, 6, self_backward, 0)
+    tick(8)
     for n in range(3):
         rows = slice(256 * n, 256 * n + 256)
-        dthird[:, rows] = back(rg, (13, 14, 15), w_qkv.at[rows, :])
+        dthird[:, rows] = back(rg, (10, 11, 12), w_qkv.at[rows, :])
+    tick(9)
 
     def store_input(rows, v):
         x_in[rows, :] = (acc[rows, :] + v).astype(BF16)
@@ -613,25 +648,27 @@
     norm_backward(
         lambda rows: x_in[rows, :].astype(F32), lambda rows: dthird[rows, :], store_input, norm_gain, sums, 0
     )
-    send(2, x_in, o_input, 64)
 
     def body(n, carry):
         red.tick(n)
         for j in range(6):
-            @pl.when(n == 2 * j)
+            @pl.when(n == 10 + j)
             def _():
                 norm_step(j, at, n_own, n_got, n_send, n_recv)
+
+        for k in range(9, 16):
+            @pl.when(n == k + 1)
+            def _():
+                send(k)
+
         return carry
 
-    lax.fori_loop(0, TRIPLES + 5, body, 0)
+    lax.fori_loop(10, red.TICKS, body, 0)
     norm_out[...] = n_own[5]
     red.drain()
-    for n in range(3):
-        for copy in swaps[n]:
-            copy.wait_send()
-    for stay, leave in gives:
-        stay.wait()
-        leave.wait()
+    for n in range(16):
+        piece(n, True).wait()
+        piece(n, False).wait()
 
 
 def layer_call(args):
@@ -648,7 +685,7 @@
             jax.ShapeDtypeStruct((8, 768), F32),
         ),
         in_specs=[anywhere, anywhere, pl.BlockSpec(memory_space=pltpu.SMEM)] + [anywhere] * 8 + [vmem] * 2,
-        out_specs=(anywhere, anywhere, anywhere, vmem, vmem),
+        out_specs=(anywhere, anywhere, anywhere, anywhere, vmem),
         scratch_shapes=[
             rows(768), pltpu.VMEM((512, 768), BF16), rows(768),
             pltpu.VMEM((768, 2304), BF16), pltpu.VMEM((768, 768), BF16), pltpu.VMEM((768, 768), BF16),
@@ -657,9 +694,9 @@
             rows(768), pltpu.VMEM((18, 256, 128), BF16), pltpu.VMEM((12, 256, 128), BF16), rows(768),
             rows(768, F32), rows(768), pltpu.VMEM((6, 256, 128), BF16), pltpu.VMEM((12, 512, 128), BF16),
             pltpu.VMEM((12, 256, 256), BF16), rows(768), rows(768, F32), rows(768),
-            rows(768), rows(768), rows(768, F32), rows(768, F32),
+            rows(768), rows(768, F32), rows(768, F32),
             pltpu.VMEM((11, 2, 384, 256), BF16),
-            pltpu.VMEM((18, 256, 768), BF16),
+            pltpu.VMEM((15, 256, 768), BF16),
             pltpu.VMEM((6, 8, 768), F32),
             pltpu.VMEM((5, 8, 768), F32),
             pltpu.SemaphoreType.DMA((5,)),
@@ -667,31 +704,91 @@
             pltpu.SemaphoreType.DMA((17,)),
             pltpu.SemaphoreType.DMA((3, 2)),
             pltpu.SemaphoreType.DMA((3, 2)),
-            pltpu.SemaphoreType.DMA((3, 2)),
-            pltpu.SemaphoreType.DMA((3, 2)),
-            pltpu.SemaphoreType.DMA((3, 2)),
+            pltpu.SemaphoreType.DMA((16,)),
+            pltpu.SemaphoreType.DMA((16,)),
+            pltpu.SemaphoreType.DMA((16,)),
         ] + Reducer.SCRATCH,
-        compiler_params=pltpu.CompilerParams(collective_id=0, has_side_effects=True, vmem_limit_bytes=60 << 20),
+        compiler_params=pltpu.CompilerParams(collective_id=0, has_side_effects=True, vmem_limit_bytes=61 << 20),
     )(*args)
 
 
+WEIGHTS = ((13, 3), (12, 1), (11, 1), (9, 2), (8, 1), (4, 4))
+
+
+def finish_kernel(layer, inputs, memories, units, norms, *refs):
+    o_layer, o_input, o_memory = refs[0:3]
+    o_weights, o_ffn_out, o_gain, o_bias = refs[3:9], refs[9], refs[10], refs[11]
+    low_input, low_memory, high_input, high_memory, blocks = refs[12:17]
+    w_bufs, ffn_buf, sem, out_sem, low_layer = refs[17:23], refs[23], refs[24], refs[25], refs[26]
+    loads = [
+        pltpu.make_async_copy(units, blocks, sem.at[0]),
+        pltpu.make_async_copy(memories, low_memory, sem.at[1]),
+        pltpu.make_async_copy(inputs, low_input, sem.at[2]),
+        pltpu.make_async_copy(layer, low_layer, sem.at[3]),
+    ]
+    for load in loads:
+        load.start()
+    stores = []
+
+    def store(src, dst):
+        copy = pltpu.make_async_copy(src, dst, out_sem.at[len(stores)])
+        copy.start()
+        stores.append(copy)
+
+    o_gain[...] = norms[0:3, :]
+    o_bias[...] = norms[3:6, :]
+    loads[0].wait()
+    for (t, count), buf, out in zip(WEIGHTS, w_bufs, o_weights):
+        for j in range(count):
+            for g in range(3):
+                buf[:, j * 384 + g * LANES : j * 384 + g * LANES + LANES] = blocks[t + j, g]
+        store(buf, out)
+    for k in range(4):
+        for g in range(3):
+            ffn_buf[48 * k : 48 * k + 48, g * LANES : g * LANES + LANES] = blocks[k, g]
+    store(ffn_buf, o_ffn_out)
+    loads[1].wait()
+    for e in range(4):
+        high_memory[e] = low_memory[e].astype(F32)
+        store(high_memory.at[e], o_memory.at[e])
+    loads[2].wait()
+    high_input[...] = low_input[...].astype(F32)
+    store(high_input, o_input)
+    loads[3].wait()
+    store(low_layer, o_layer)
+    for copy in stores:
+        copy.wait()
+
+
+def finish_call(layer, inputs, memories, units, norms):
+    anywhere = pl.BlockSpec(memory_space=pl.ANY)
+    vmem = pl.BlockSpec(memory_space=pltpu.VMEM)
+    widths = [count * 384 for _, count in WEIGHTS]
+    return pl.pallas_call(
+        finish_kernel,
+        out_shape=(
+            jax.ShapeDtypeStruct(layer.shape, BF16),
+            jax.ShapeDtypeStruct(inputs.shape, F32),
+            jax.ShapeDtypeStruct(memories.shape, F32),
+            *[jax.ShapeDtypeStruct((48, w), F32) for w in widths],
+            jax.ShapeDtypeStruct((192, 384), F32),
+            jax.ShapeDtypeStruct((3, 768), F32),
+            jax.ShapeDtypeStruct((3, 768), F32),
+        ),
+        in_specs=[anywhere] * 4 + [vmem],
+        out_specs=(anywhere,) * 10 + (vmem, vmem),
+        scratch_shapes=[
+            pltpu.VMEM(inputs.shape, BF16), pltpu.VMEM(memories.shape, BF16),
+            pltpu.VMEM(inputs.shape, F32), pltpu.VMEM(memories.shape, F32), pltpu.VMEM(units.shape, F32),
+            *[pltpu.VMEM((48, w), F32) for w in widths], pltpu.VMEM((192, 384), F32),
+            pltpu.SemaphoreType.DMA((4,)), pltpu.SemaphoreType.DMA((13,)), pltpu.VMEM(layer.shape, BF16),
+        ],
+        compiler_params=pltpu.CompilerParams(vmem_limit_bytes=60 << 20),
+    )(layer, inputs, memories, units, norms)
+
+
 def per_device_paired(*args):
-    layer_out, input_grad, memory_grad, units, norms = layer_call(args)
-    grads = gather_outputs(units)
-    return (
-        layer_out,
-        input_grad.astype(F32),
-        memory_grad.astype(F32),
-        grads["self_qkv"],
-        grads["self_out"],
-        grads["cross_query"],
-        grads["cross_kv"],
-        grads["cross_out"],
-        grads["ffn_in"],
-        grads["ffn_out"],
-        norms[0:3],
-        norms[3:6],
-    )
+    return finish_call(*layer_call(args))
 
 def layer_norm(x, gain, shift):
     center = jnp.mean(x, axis=-1, keepdims=True)

time: 158 us -> 133 us (0.84)
  Pallas kernels: 147 us -> 132 us
  local copies, waits for them, and re-layouts: 7.73 us -> 0 us
  other arithmetic: 2.21 us -> 0 us
    pallas_call x1, Pallas kernels: 147 us -> 127 us  [layer_call(): pl.pallas_call(layer_kernel, out_shape=(jax.ShapeDtypeStruct((4, 64, 768)...]
    pallas_call x0 -> x1, Pallas kernels: none -> 4.69 us  [finish_call(): pl.pallas_call(finish_kernel, out_shape=(jax.ShapeDtypeStruct(layer.shape...]
    reshape x4 -> x0, local copies, waits for them, and re-layouts: 3.08 us -> none  [assemble(): return jnp.transpose(block, (2, 0, 1, 3)).reshape(48, count * 384)]
    unnamed x13 -> x0, local copies, waits for them, and re-layouts: 2.29 us -> none
    convert_element_type x2 -> x0, other arithmetic: 2.21 us -> none  [the longest x1 1.27 us: per_device_paired(): memory_grad.astype(F32)]
    transpose x11 -> x0, local copies, waits for them, and re-layouts: 1.75 us -> none  [the longest x9 1.56 us: assemble(): return jnp.transpose(block, (2, 0, 1, 3)).reshape(48, count * 384)]
where the time goes in v1:
time: 133 us
  Pallas kernels  132 us (99%)
    pallas_call x1, Pallas kernels, layer_call(): pl.pallas_call(layer_kernel, out_shape=(jax.ShapeDtypeStruct((4, 64, 768)...  127 us
    pallas_call x1, Pallas kernels, finish_call(): pl.pallas_call(finish_kernel, out_shape=(jax.ShapeDtypeStruct(layer.shape...  4.69 us

profile of v1, /device:TPU:0, one launch (start us, length us, event | category | flops | bytes accessed | tf_op | source)
XLA Modules:
  0.0 132.7 jit_solution(13043976579016596891)
XLA Ops:
  0.6 127.2 %shard_map.220 = (bf16[4,64,768]{2,1,0:T(8,128)(2,1)}, bf16[4,64,768]{2,1,0:T(8,128)(2,1)}, bf16[4,128,768]{2,1,0:T(8,128)(2,1)}, f32[16,3,48,128]{3,2,1,0:T(8,128)}, f32[8,768]{1,0:T(8,128)}) custom-call(bf16[4,64,768]{2,1,0:T(8,128)(2,1)} %dec_input.1, bf16[4,128,768]{2,1,0:T(8,128)(2,1)} %memory.1, s32[4]{0:T(128)} %src_len.1, ...), custom_call_target="tpu_custom_call" | custom-call | tf_op jit(solution)/shard_map/pallas_call | solution.py:678
  127.8 4.7 %shard_map.221 = (bf16[4,64,768]{2,1,0:T(8,128)(2,1)}, f32[4,64,768]{2,1,0:T(8,128)}, f32[4,128,768]{2,1,0:T(8,128)}, f32[48,1152]{1,0:T(8,128)}, f32[48,384]{1,...) custom-call(bf16[4,64,768]{2,1,0:T(8,128)(2,1)} %get-tuple-element.1, ...), custom_call_target="tpu_custom_call" | custom-call | tf_op jit(solution)/shard_map/pallas_call | solution.py:767

commit v2 on v1

--- a/solution.py
+++ b/solution.py
@@ -38,8 +38,8 @@
     pl.semaphore_wait(barrier, 5)
 
 
-LEFT = (0, 1, 2, 3, 4, 4, 4, 4, 5, 6, 6, 8, 9, 10, 10, 10)
-RIGHT = (0, 0, 0, 0, 1, 2, 3, 4, 5, 6, 7, 8, 9, 10, 11, 12)
+LEFT = (4, 4, 4, 4, 0, 1, 2, 3, 5, 6, 6, 8, 9, 10, 10, 10)
+RIGHT = (1, 2, 3, 4, 0, 0, 0, 0, 5, 6, 7, 8, 9, 10, 11, 12)
 
 
 def look_up(table, t):
@@ -278,10 +278,10 @@
     return jnp.concatenate([jnp.where(first, tile, zero), jnp.where(first, zero, tile)], axis=0)
 
 
-def side_by_side(stacked):
-    rows = stacked.shape[0] // 2
-    first = lax.broadcasted_iota(jnp.int32, (rows, stacked.shape[1]), 1) < HEAD_DIM
-    return jnp.where(first, stacked[:rows], stacked[rows:])
+def upright(sideways):
+    rows = sideways.shape[1] // 2
+    own = jnp.concatenate([sideways[:HEAD_DIM, :rows], sideways[HEAD_DIM:, rows:]], axis=0)
+    return own.T
 
 
 def dot(a, b, over):
@@ -293,23 +293,31 @@
 ROWS = ((0,), (0,))
 
 
-def attend(q, k, v, allowed):
-    scores = jnp.where(allowed, dot(two_heads(q), k, LAST), -1e30)
-    raised = jnp.exp(scores - jnp.max(scores, axis=-1, keepdims=True))
-    weights = (raised * (1.0 / jnp.sum(raised, axis=-1, keepdims=True))).astype(BF16)
-    return weights, side_by_side(dot(weights, v, PLAIN)).astype(BF16)
-
-
-def attend_back(q, k, v, weights, dc):
-    stacked = two_heads(dc)
-    dv = dot(weights, stacked, ROWS)
-    dweights = dot(stacked, v, LAST)
-    probs = weights.astype(F32)
-    terms = probs * dweights
-    dscores = (terms - probs * jnp.sum(terms, axis=-1, keepdims=True)).astype(BF16)
-    dq = side_by_side(dot(dscores, k, PLAIN)) * (1.0 / math.sqrt(HEAD_DIM))
-    dk = dot(dscores, two_heads(q), ROWS)
-    return dq.astype(BF16), dk.astype(BF16), dv.astype(BF16)
+def attend(items):
+    scores = [jnp.where(allowed, dot(k, two_heads(q), LAST), -1e30) for q, k, _, allowed in items]
+    raised = [jnp.exp(s - jnp.max(s, axis=0, keepdims=True)) for s in scores]
+    weights = [(r * (1.0 / jnp.sum(r, axis=0, keepdims=True))).astype(BF16) for r in raised]
+    contexts = [upright(dot(item[2], w, ROWS).astype(BF16)) for w, item in zip(weights, items)]
+    return list(zip(weights, contexts))
+
+
+def attend_back(items):
+    stacked = [two_heads(item[4]) for item in items]
+    dweights = [dot(item[2], s, LAST) for item, s in zip(items, stacked)]
+    dvs = [dot(item[3], s, PLAIN).astype(BF16) for item, s in zip(items, stacked)]
+    dscores = []
+    for item, d in zip(items, dweights):
+        probs = item[3].astype(F32)
+        terms = probs * d
+        dscores.append((terms - probs * jnp.sum(terms, axis=0, keepdims=True)).astype(BF16))
+    dqs = [upright((dot(item[1], d, ROWS) * (1.0 / math.sqrt(HEAD_DIM))).astype(BF16)) for item, d in zip(items, dscores)]
+    dks = [dot(d, two_heads(item[0]), PLAIN).astype(BF16) for item, d in zip(items, dscores)]
+    return list(zip(dqs, dks, dvs))
+
+
+def in_groups(pairs, size, body):
+    for n in range(0, len(pairs), size):
+        body(pairs[n : n + size])
 
 
 def column(slot, h, g):
@@ -351,8 +359,9 @@
     for load in loads:
         load.start()
 
-    def ffn_load(q):
-        slot = q % 2
+    def ffn_load(n):
+        slot = n % 2
+        q = (n % 2) * 2 + n // 2
         cols = pl.ds(pl.multiple_of(q * 768, 768), 768)
         return (
             pltpu.make_async_copy(ffn_in.at[:, cols], w_in.at[slot], load_sem.at[7 + slot]),
@@ -405,30 +414,30 @@
     norm_forward(lambda rows: x_in[rows, :].astype(F32), first, norm_gain, norm_bias, 0)
     loads[0].wait()
 
-    def project_qkv(n, carry):
-        cols = pl.ds(pl.multiple_of(256 * n, 256), 256)
-        out = jnp.dot(first[...], w_qkv[:, cols], preferred_element_type=F32)
-        out = (out.astype(BF16) * jnp.where(n < 3, scale, 1.0).astype(BF16)).astype(BF16)
+    for n in range(9):
+        out = jnp.dot(first[...], w_qkv[:, 256 * n : 256 * n + 256], preferred_element_type=F32)
+        out = (out * scale if n < 3 else out).astype(BF16)
         qkv[2 * n] = out[:, 0:LANES]
         qkv[2 * n + 1] = out[:, LANES:256]
-        return carry
-
-    lax.fori_loop(0, 9, project_qkv, 0)
 
     def pair(e, p):
-        return slice(e * 128, e * 128 + 128), pl.ds(pl.multiple_of(p * LANES, LANES), LANES)
-
-    def self_forward(p, carry):
-        q_at = lax.broadcasted_iota(jnp.int32, (256, 128), 0) % 128
-        k_at = lax.broadcasted_iota(jnp.int32, (256, 128), 1)
-        for e in range(2):
-            rows, lanes = pair(e, p)
-            weights, context = attend(qkv[p, rows, :], qkv[6 + p, rows, :], qkv[12 + p, rows, :], q_at >= k_at)
+        return slice(e * 128, e * 128 + 128), slice(p * LANES, p * LANES + LANES)
+
+    pairs = [(e, p) for p in range(6) for e in range(2)]
+
+    def self_operands(e, p):
+        rows, _ = pair(e, p)
+        return qkv[p, rows, :], qkv[6 + p, rows, :], qkv[12 + p, rows, :]
+
+    def self_forward(group):
+        k_at = lax.broadcasted_iota(jnp.int32, (128, 256), 0)
+        q_at = lax.broadcasted_iota(jnp.int32, (128, 256), 1) % 128
+        results = attend([(*self_operands(e, p), q_at >= k_at) for e, p in group])
+        for (e, p), (weights, context) in zip(group, results):
             p_self[6 * e + p] = weights
-            ctx_self[rows, lanes] = context
-        return carry
-
-    lax.fori_loop(0, 6, self_forward, 0)
+            ctx_self[pair(e, p)] = context
+
+    in_groups(pairs, 4, self_forward)
 
     loads[1].wait()
     for n in range(3):
@@ -439,34 +448,29 @@
     loads[3].wait()
     for n in range(3):
         out = jnp.dot(second[...], w_query[:, 256 * n : 256 * n + 256], preferred_element_type=F32)
-        out = (out.astype(BF16) * jnp.asarray(scale, BF16)).astype(BF16)
+        out = (out * scale).astype(BF16)
         qx[2 * n] = out[:, 0:LANES]
         qx[2 * n + 1] = out[:, LANES:256]
     loads[2].wait()
     arrived(1)
 
-    def project_kv(n, carry):
-        cols = pl.ds(pl.multiple_of(256 * n, 256), 256)
-        out = jnp.dot(mem[...], w_kv[:, cols], preferred_element_type=F32).astype(BF16)
+    for n in range(6):
+        out = jnp.dot(mem[...], w_kv[:, 256 * n : 256 * n + 256], preferred_element_type=F32).astype(BF16)
         kv[2 * n] = out[:, 0:LANES]
         kv[2 * n + 1] = out[:, LANES:256]
-        return carry
-
-    lax.fori_loop(0, 6, project_kv, 0)
-
-    def cross_rows(e):
-        return slice(e * 256, e * 256 + 256)
-
-    def cross_forward(p, carry):
-        for e in range(2):
-            rows, lanes = pair(e, p)
-            allowed = lax.broadcasted_iota(jnp.int32, (256, 256), 1) < src_len[2 * y + e]
-            weights, context = attend(qx[p, rows, :], kv[p, cross_rows(e), :], kv[6 + p, cross_rows(e), :], allowed)
+
+    def cross_operands(e, p):
+        rows, keys = pair(e, p)[0], slice(e * 256, e * 256 + 256)
+        return qx[p, rows, :], kv[p, keys, :], kv[6 + p, keys, :]
+
+    def cross_forward(group):
+        k_at = lax.broadcasted_iota(jnp.int32, (256, 256), 0)
+        results = attend([(*cross_operands(e, p), k_at < src_len[2 * y + e]) for e, p in group])
+        for (e, p), (weights, context) in zip(group, results):
             p_cross[6 * e + p] = weights
-            ctx_cross[rows, lanes] = context
-        return carry
-
-    lax.fori_loop(0, 6, cross_forward, 0)
+            ctx_cross[pair(e, p)] = context
+
+    in_groups(pairs, 4, cross_forward)
 
     loads[4].wait()
     for n in range(3):
@@ -487,15 +491,16 @@
     dthird[...] = jnp.zeros_like(dthird)
     root = math.sqrt(2.0 / math.pi)
 
-    def feed(q, carry):
-        slot = q % 2
-
-        @pl.when(q < 3)
+    def feed(n, carry):
+        slot = n % 2
+        q = (n % 2) * 2 + n // 2
+
+        @pl.when(n < 3)
         def _():
-            for load in ffn_load(q + 1):
+            for load in ffn_load(n + 1):
                 load.start()
 
-        for load in ffn_load(q):
+        for load in ffn_load(n):
             load.wait()
 
         def up_tile(tile):
@@ -526,8 +531,6 @@
                 lt[k, i % 2, rows, :] = flipped[192 * i + 48 * k : 192 * i + 48 * k + 48, :]
         return carry
 
-    lax.fori_loop(0, 4, feed, 0)
-
     PIECES = (
         [(third, o_layer, 64, e, r) for e in range(2) for r in (0, 32)]
         + [(mem, o_memory, 128, e, r) for e in range(2) for r in (0, 32, 64, 96)]
@@ -551,11 +554,15 @@
 
     def tick(n):
         red.tick(n)
-        if n:
-            send(n - 1)
-
+        if n >= 3:
+            send(n - 3)
+
+    lax.fori_loop(0, 2, feed, 0)
+    store_left(lt, 4, third[...].T)
     tick(0)
-    store_left(lt, 4, third[...].T)
+    tick(1)
+    lax.fori_loop(2, 4, feed, 0)
+    tick(2)
 
     third[...] = (hidden2[...] + acc[...]).astype(BF16)
 
@@ -570,7 +577,7 @@
         lambda rows, v: store_grad(rows, og[rows, :].astype(F32) + v), norm_gain, sums, 2,
     )
     spread(5, acc)
-    tick(1)
+    tick(3)
     store_left(lt, 5, ctx_cross[...].T)
     dc = active
 
@@ -581,20 +588,18 @@
 
     context_grad(5, w_cross)
 
-    def cross_backward(p, carry):
-        for e in range(2):
-            rows, lanes = pair(e, p)
-            dq, dk, dv = attend_back(qx[p, rows, :], kv[p, cross_rows(e), :], kv[6 + p, cross_rows(e), :], p_cross[6 * e + p], dc[rows, lanes])
-            h, j, g = p // 3, p // 3, p % 3
-            rg[8, rows, pl.ds(pl.multiple_of(256 * g + LANES * h, LANES), LANES)] = dq
-            rg[column(6 + 7 * e + j, 0, g)] = dk
-            rg[column(6 + 7 * e + j, 1, g)] = dv
-        return carry
-
-    tick(2)
-    lax.fori_loop(0, 3, cross_backward, 0)
-    tick(3)
-    lax.fori_loop(3, 6, cross_backward, 0)
+    def cross_backward(group):
+        results = attend_back([(*cross_operands(e, p), p_cross[6 * e + p], dc[pair(e, p)]) for e, p in group])
+        for (e, p), (dq, dk, dv) in zip(group, results):
+            j, g = p // 3, p % 3
+            rg[8, pair(e, p)[0], 256 * g + LANES * j : 256 * g + LANES * j + LANES] = dq
+            rg[6 + 7 * e + j, :, 256 * g : 256 * g + LANES] = dk
+            rg[6 + 7 * e + j, :, 256 * g + LANES : 256 * g + 256] = dv
+
+    tick(4)
+    in_groups(pairs[:6], 3, cross_backward)
+    tick(5)
+    in_groups(pairs[6:], 3, cross_backward)
 
     store_left(lt, 6, mem[0:256, :].T)
     store_left(lt, 7, mem[256:512, :].T)
@@ -605,42 +610,39 @@
             mem[256 * e : 256 * e + 256, rows] = back(rg, (6 + 7 * e, 7 + 7 * e), w_kv.at[rows, :]).astype(BF16)
 
     memory_rows(0)
-    tick(4)
+    tick(6)
     memory_rows(1)
     for n in range(3):
         rows = slice(256 * n, 256 * n + 256)
         dthird[:, rows] = back(rg, (8,), w_query.at[rows, :])
-    tick(5)
+    tick(7)
     norm_backward(
         lambda rows: hidden1[rows, :], lambda rows: dthird[rows, :],
         lambda rows, v: store_grad(rows, acc[rows, :] + v), norm_gain, sums, 1,
     )
     spread(9, acc)
     context_grad(9, w_self)
-    tick(6)
+    tick(8)
     store_left(lt, 8, second[...].T)
     store_left(lt, 9, ctx_self[...].T)
     store_left(lt, 10, first[...].T)
 
-    def self_backward(p, carry):
-        for e in range(2):
-            rows, lanes = pair(e, p)
-            dq, dk, dv = attend_back(qkv[p, rows, :], qkv[6 + p, rows, :], qkv[12 + p, rows, :], p_self[6 * e + p], dc[rows, lanes])
-            for n, value in enumerate((dq, dk, dv)):
+    def self_backward(group):
+        results = attend_back([(*self_operands(e, p), p_self[6 * e + p], dc[pair(e, p)]) for e, p in group])
+        for (e, p), values in zip(group, results):
+            for n, value in enumerate(values):
                 tile = 6 * n + p
-                h = tile // 9
-                j = (tile % 9) // 3
-                rg[10 + j, rows, pl.ds(pl.multiple_of(256 * (tile % 3) + LANES * h, LANES), LANES)] = value
-        return carry
-
-    lax.fori_loop(0, 3, self_backward, 0)
-    tick(7)
-    lax.fori_loop(3, 6, self_backward, 0)
-    tick(8)
+                lane = 256 * (tile % 3) + LANES * (tile // 9)
+                rg[10 + (tile % 9) // 3, pair(e, p)[0], lane : lane + LANES] = value
+
+    in_groups(pairs[:6], 3, self_backward)
+    tick(9)
+    in_groups(pairs[6:], 3, self_backward)
+    tick(10)
     for n in range(3):
         rows = slice(256 * n, 256 * n + 256)
         dthird[:, rows] = back(rg, (10, 11, 12), w_qkv.at[rows, :])
-    tick(9)
+    tick(11)
 
     def store_input(rows, v):
         x_in[rows, :] = (acc[rows, :] + v).astype(BF16)
@@ -652,18 +654,18 @@
     def body(n, carry):
         red.tick(n)
         for j in range(6):
-            @pl.when(n == 10 + j)
+            @pl.when(n == 12 + j)
             def _():
                 norm_step(j, at, n_own, n_got, n_send, n_recv)
 
         for k in range(9, 16):
-            @pl.when(n == k + 1)
+            @pl.when(n == k + 3)
             def _():
                 send(k)
 
         return carry
 
-    lax.fori_loop(10, red.TICKS, body, 0)
+    lax.fori_loop(12, red.TICKS, body, 0)
     norm_out[...] = n_own[5]
     red.drain()
     for n in range(16):
@@ -691,7 +693,7 @@
             pltpu.VMEM((768, 2304), BF16), pltpu.VMEM((768, 768), BF16), pltpu.VMEM((768, 768), BF16),
             pltpu.VMEM((768, 1536), BF16), pltpu.VMEM((768, 768), BF16),
             pltpu.VMEM((2, 768, 768), BF16), pltpu.VMEM((2, 768, 768), BF16),
-            rows(768), pltpu.VMEM((18, 256, 128), BF16), pltpu.VMEM((12, 256, 128), BF16), rows(768),
+            rows(768), pltpu.VMEM((18, 256, 128), BF16), pltpu.VMEM((12, 128, 256), BF16), rows(768),
             rows(768, F32), rows(768), pltpu.VMEM((6, 256, 128), BF16), pltpu.VMEM((12, 512, 128), BF16),
             pltpu.VMEM((12, 256, 256), BF16), rows(768), rows(768, F32), rows(768),
             rows(768), rows(768, F32), rows(768, F32),
@@ -712,7 +714,7 @@
     )(*args)
 
 
-WEIGHTS = ((13, 3), (12, 1), (11, 1), (9, 2), (8, 1), (4, 4))
+WEIGHTS = ((13, 3), (12, 1), (11, 1), (9, 2), (8, 1), (0, 4))
 
 
 def finish_kernel(layer, inputs, memories, units, norms, *refs):
@@ -745,7 +747,7 @@
         store(buf, out)
     for k in range(4):
         for g in range(3):
-            ffn_buf[48 * k : 48 * k + 48, g * LANES : g * LANES + LANES] = blocks[k, g]
+            ffn_buf[48 * k : 48 * k + 48, g * LANES : g * LANES + LANES] = blocks[4 + k, g]
     store(ffn_buf, o_ffn_out)
     loads[1].wait()
     for e in range(4):

time: 133 us -> 125 us (0.940)
  Pallas kernels: 132 us -> 124 us
    pallas_call x1, Pallas kernels: 127 us -> 119 us  [layer_call(): pl.pallas_call(layer_kernel, out_shape=(jax.ShapeDtypeStruct((4, 64, 768)...]
where the time goes in v2:
time: 125 us
  Pallas kernels  124 us (99%)
    pallas_call x1, Pallas kernels, layer_call(): pl.pallas_call(layer_kernel, out_shape=(jax.ShapeDtypeStruct((4, 64, 768)...  119 us
    pallas_call x1, Pallas kernels, finish_call(): pl.pallas_call(finish_kernel, out_shape=(jax.ShapeDtypeStruct(layer.shape...  4.69 us

profile of v2, /device:TPU:0, one launch (start us, length us, event | category | flops | bytes accessed | tf_op | source)
XLA Modules:
  0.0 124.6 jit_solution(17779225518472825973)
XLA Ops:
  0.6 119.1 %shard_map.220 = (bf16[4,64,768]{2,1,0:T(8,128)(2,1)}, bf16[4,64,768]{2,1,0:T(8,128)(2,1)}, bf16[4,128,768]{2,1,0:T(8,128)(2,1)}, f32[16,3,48,128]{3,2,1,0:T(8,128)}, f32[8,768]{1,0:T(8,128)}) custom-call(bf16[4,64,768]{2,1,0:T(8,128)(2,1)} %dec_input.1, bf16[4,128,768]{2,1,0:T(8,128)(2,1)} %memory.1, s32[4]{0:T(128)} %src_len.1, ...), custom_call_target="tpu_custom_call" | custom-call | tf_op jit(solution)/shard_map/pallas_call | solution.py:680
  119.8 4.7 %shard_map.221 = (bf16[4,64,768]{2,1,0:T(8,128)(2,1)}, f32[4,64,768]{2,1,0:T(8,128)}, f32[4,128,768]{2,1,0:T(8,128)}, f32[48,1152]{1,0:T(8,128)}, f32[48,384]{1,...) custom-call(bf16[4,64,768]{2,1,0:T(8,128)(2,1)} %get-tuple-element.1, ...), custom_call_target="tpu_custom_call" | custom-call | tf_op jit(solution)/shard_map/pallas_call | solution.py:769
